TPU v7x, 32 devices: a whole 2x2x4 slice. The times are simulated.
32 devices in a mesh: dp: 16 (over z, y, core), tensor: 2 (over x).
Axes of the slice: x: 2, y: 2, z: 4, core: 2. Of those that a mesh axis runs over, the one named last changes fastest.
Arguments:
- hidden_in: bfloat16 [4096, 1024], P(('dp', 'tensor')), may hold values from -6 to 6
- out_grad: bfloat16 [4096, 1024], P(('dp', 'tensor')), may hold values from -6 to 6
- span_start: int32 [16, 2], P('dp'), may hold values from 0 to 240, as said below
- span_length: int32 [16, 2], P('dp'), may hold values from 16 to 128
- attn_gain: bfloat16 [1024], P(('dp', 'tensor')), may hold values from 0.099609375 to 1.8984375
- attn_shift: bfloat16 [1024], P(('dp', 'tensor')), may hold values from -3 to 3
- mlp_gain: bfloat16 [1024], P(('dp', 'tensor')), may hold values from 0.099609375 to 1.8984375
- mlp_shift: bfloat16 [1024], P(('dp', 'tensor')), may hold values from -3 to 3
- qkv_weight: bfloat16 [1024, 3, 1024], P('dp', None, 'tensor'), may hold values from -0.1875 to 0.1875
- qkv_bias: bfloat16 [3, 1024], P(None, ('tensor', 'dp')), may hold values from -3 to 3
- dense_weight: bfloat16 [1024, 1024], P(('tensor', 'dp')), may hold values from -1.5 to 1.5
- dense_bias: bfloat16 [1024], P(('dp', 'tensor')), may hold values from -3 to 3
- up_weight: bfloat16 [1024, 4096], P('dp', 'tensor'), may hold values from -0.1875 to 0.1875
- up_bias: bfloat16 [4096], P(('tensor', 'dp')), may hold values from -3 to 3
- down_weight: bfloat16 [4096, 1024], P(('tensor', 'dp')), may hold values from -0.09375 to 0.09375
- down_bias: bfloat16 [1024], P(('dp', 'tensor')), may hold values from -3 to 3
Outputs:
- layer_out: bfloat16 [4096, 1024], P(('dp', 'tensor'))
- input_grad: bfloat16 [4096, 1024], P(('dp', 'tensor'))
- attn_gain_grad: float32 [1024], P(('dp', 'tensor'))
- attn_shift_grad: float32 [1024], P(('dp', 'tensor'))
- mlp_gain_grad: float32 [1024], P(('dp', 'tensor'))
- mlp_shift_grad: float32 [1024], P(('dp', 'tensor'))
- qkv_weight_grad: float32 [1024, 3, 1024], P('dp', None, 'tensor')
- qkv_bias_grad: float32 [3, 1024], P(None, ('tensor', 'dp'))
- dense_weight_grad: float32 [1024, 1024], P(('tensor', 'dp'))
- dense_bias_grad: float32 [1024], P(('dp', 'tensor'))
- up_weight_grad: float32 [1024, 4096], P('dp', 'tensor')
- up_bias_grad: float32 [4096], P(('tensor', 'dp'))
- down_weight_grad: float32 [4096, 1024], P(('tensor', 'dp'))
- down_bias_grad: float32 [1024], P(('dp', 'tensor'))
Inputs may be any that keep to these rules, and one draw needn't show every extreme that they name: `span_start`: span slot k of a sequence lies inside its positions k * 128 to (k + 1) * 128 - 1.
All inputs are finite; a program needn't handle non-finite values.
Results may differ from a plain program's by a relative error of at most 0.011.
Values may be sent and summed in bfloat16 or wider, within the bound.
A program may use at most 128 MiB of HBM per device.

v0:
```python
import jax
import jax.numpy as jnp
from jax import lax
from jax.sharding import PartitionSpec as P

HD = 64
ROT = 16


NORM_EPS = 1e-05
NEG_FILL = -1000000000.0


def layer_norm(rows_in, gain_vec, shift_vec):
    mean_row = jnp.mean(rows_in, axis=-1, keepdims=True)
    centred = rows_in - mean_row
    spread = jnp.mean(centred * centred, axis=-1, keepdims=True)
    return centred * lax.rsqrt(spread + NORM_EPS) * gain_vec + shift_vec


def rotary_tables(length):
    position = jnp.arange(length, dtype=jnp.float32)
    rates = 10000.0 ** (-jnp.arange(ROT // 2, dtype=jnp.float32) * (2.0 / ROT))
    angles = position[:, None] * rates[None, :]
    angles = jnp.concatenate([angles, angles], axis=-1)[:, None, :]
    return (jnp.cos(angles), jnp.sin(angles))


def rotate(field_in, cosine, sines):
    turned = field_in[..., :ROT]
    first_half = turned[..., : ROT // 2]
    second_half = turned[..., ROT // 2 :]
    swapped = jnp.concatenate([-second_half, first_half], axis=-1)
    return jnp.concatenate([turned * cosine + swapped * sines, field_in[..., ROT:]], axis=-1)


def gelu_exact(values_in):
    return jax.nn.gelu(values_in, approximate=False)


def shards(
    hidden_in,
    out_grad,
    span_start,
    span_length,
    attn_gain,
    attn_shift,
    mlp_gain,
    mlp_shift,
    qkv_weight,
    qkv_bias,
    dense_weight,
    dense_bias,
    up_weight,
    up_bias,
    down_weight,
    down_bias,
):
    local_rows = hidden_in.shape[0]
    length = local_rows * lax.axis_size("tensor")
    block_rows = min(512, length)
    block_count = length // block_rows
    score_scale = HD ** (-0.5)
    small_full = (
        lax.all_gather(attn_gain, ("dp", "tensor"), axis=0, tiled=True),
        lax.all_gather(attn_shift, ("dp", "tensor"), axis=0, tiled=True),
        lax.all_gather(mlp_gain, ("dp", "tensor"), axis=0, tiled=True),
        lax.all_gather(mlp_shift, ("dp", "tensor"), axis=0, tiled=True),
        lax.all_gather(dense_bias, ("dp", "tensor"), axis=0, tiled=True),
        lax.all_gather(down_bias, ("dp", "tensor"), axis=0, tiled=True),
    )
    small_vecs = [item.astype(jnp.float32) for item in small_full]
    own_rows = hidden_in.astype(jnp.float32)
    normed_attn = layer_norm(own_rows, small_vecs[0], small_vecs[1]).astype(jnp.bfloat16)
    normed_mlp = layer_norm(own_rows, small_vecs[2], small_vecs[3]).astype(jnp.bfloat16)
    attn_full, mlp_full = (
        lax.all_gather(normed_attn, "tensor", axis=0, tiled=True),
        lax.all_gather(normed_mlp, "tensor", axis=0, tiled=True),
    )
    full_qkv, full_qkv_bias, full_dense, full_up, full_up_bias, full_down = (
        lax.all_gather(qkv_weight, "dp", axis=0, tiled=True),
        lax.all_gather(qkv_bias, "dp", axis=1, tiled=True),
        lax.all_gather(dense_weight, "dp", axis=0, tiled=True),
        lax.all_gather(up_weight, "dp", axis=0, tiled=True),
        lax.all_gather(up_bias, "dp", axis=0, tiled=True),
        lax.all_gather(down_weight, "dp", axis=0, tiled=True),
    )
    model_width = full_qkv.shape[0]
    head_cols = full_qkv.shape[2]
    local_heads = head_cols // HD
    projected = jnp.dot(
        attn_full, full_qkv.reshape(model_width, 3 * head_cols), preferred_element_type=jnp.float32
    )
    projected = projected + full_qkv_bias.reshape(3 * head_cols).astype(jnp.float32)
    projected = projected.reshape(length, 3, local_heads, HD)
    cosine, sines = rotary_tables(length)
    query_rows = rotate(projected[:, 0], cosine, sines).astype(jnp.bfloat16)
    key_rows = rotate(projected[:, 1], cosine, sines).astype(jnp.bfloat16)
    value_rows = projected[:, 2].astype(jnp.bfloat16)
    position = jnp.arange(length, dtype=jnp.int32)
    starts_here = span_start[0]
    lengths_here = span_length[0]
    inside = (position[None, :] >= starts_here[:, None]) & (
        position[None, :] < (starts_here + lengths_here)[:, None]
    )
    marks = (jnp.arange(starts_here.shape[0], dtype=jnp.int32) + 1)[:, None]
    labels = jnp.sum(jnp.where(inside, marks, 0), axis=0)

    def block_scores(first_row, query_block):
        raw_scores = (
            jnp.einsum("qhe,khe->hqk", query_block, key_rows, preferred_element_type=jnp.float32)
            * score_scale
        )
        row_pos = first_row + jnp.arange(block_rows, dtype=jnp.int32)
        allowed = (position[None, :] <= row_pos[:, None]) | (labels[:, None] == labels[None, :]) & (
            labels[:, None] > 0
        )
        return jnp.where(allowed[None], raw_scores, NEG_FILL)

    def attend(first_row):
        scores = block_scores(first_row, query_rows)
        row_top = jnp.max(scores, axis=-1, keepdims=True)
        exponent = jnp.exp(scores - row_top)
        summed = jnp.sum(exponent, axis=-1, keepdims=True)
        prob_low = (exponent / summed).astype(jnp.bfloat16)
        context_block = jnp.einsum(
            "hqk,khe->qhe", prob_low, value_rows, preferred_element_type=jnp.float32
        )
        return (context_block.astype(jnp.bfloat16), (row_top + jnp.log(summed))[..., 0])

    block_starts = jnp.arange(block_count, dtype=jnp.int32) * block_rows
    context_blocks, lse_blocks = lax.map(attend, block_starts)
    context = context_blocks.reshape(length, head_cols)
    attn_part = jnp.dot(context, full_dense, preferred_element_type=jnp.float32)
    attn_mixed = lax.psum_scatter(
        attn_part.astype(jnp.bfloat16), "tensor", scatter_dimension=0, tiled=True
    ).astype(jnp.float32)
    hidden = jnp.dot(mlp_full, full_up, preferred_element_type=jnp.float32) + full_up_bias.astype(
        jnp.float32
    )
    active = gelu_exact(hidden).astype(jnp.bfloat16)
    mlp_part = jnp.dot(active, full_down, preferred_element_type=jnp.float32)
    mixed_rows = attn_mixed + lax.psum_scatter(
        mlp_part.astype(jnp.bfloat16), "tensor", scatter_dimension=0, tiled=True
    ).astype(jnp.float32)
    layer_out = (own_rows + mixed_rows + small_vecs[4] + small_vecs[5]).astype(jnp.bfloat16)
    cot_full = lax.all_gather(out_grad, "tensor", axis=0, tiled=True)
    full_qkv, full_dense, full_up, full_down = (
        lax.all_gather(qkv_weight, "dp", axis=0, tiled=True),
        lax.all_gather(dense_weight, "dp", axis=0, tiled=True),
        lax.all_gather(up_weight, "dp", axis=0, tiled=True),
        lax.all_gather(down_weight, "dp", axis=0, tiled=True),
    )
    down_grad = jnp.einsum("lf,ld->fd", active, cot_full, preferred_element_type=jnp.float32)
    dense_grad = jnp.einsum("le,ld->ed", context, cot_full, preferred_element_type=jnp.float32)
    active_grad = jnp.einsum("ld,fd->lf", cot_full, full_down, preferred_element_type=jnp.float32)
    hidden_grad = jax.vjp(gelu_exact, hidden)[1](active_grad)[0].astype(jnp.bfloat16)
    up_grad = jnp.einsum("ld,lf->df", mlp_full, hidden_grad, preferred_element_type=jnp.float32)
    up_bias_grad = jnp.sum(hidden_grad, axis=0, dtype=jnp.float32)
    mlp_in_grad = jnp.einsum("lf,df->ld", hidden_grad, full_up, preferred_element_type=jnp.float32)
    context_grad = jnp.einsum("ld,ed->le", cot_full, full_dense, preferred_element_type=jnp.float32)
    context_grad = context_grad.astype(jnp.bfloat16).reshape(length, local_heads, HD)

    def attend_back(carried, inputs):
        key_acc, value_acc = carried
        first_row, lse_block = inputs
        scores = block_scores(first_row, query_rows)
        prob_rows = jnp.exp(scores - lse_block[..., None])
        prob_low = prob_rows.astype(jnp.bfloat16)
        value_acc = value_acc + jnp.einsum(
            "hqk,qhe->khe", prob_low, context_grad, preferred_element_type=jnp.float32
        )
        prob_grad = jnp.einsum(
            "qhe,khe->hqk", context_grad, value_rows, preferred_element_type=jnp.float32
        )
        score_grad = prob_rows * (
            prob_grad - jnp.sum(prob_grad * prob_rows, axis=-1, keepdims=True)
        )
        score_grad = score_grad.astype(jnp.bfloat16)
        query_grad = (
            jnp.einsum("hqk,khe->qhe", score_grad, key_rows, preferred_element_type=jnp.float32)
            * score_scale
        )
        key_acc = (
            key_acc
            + jnp.einsum("hqk,qhe->khe", score_grad, query_rows, preferred_element_type=jnp.float32)
            * score_scale
        )
        return ((key_acc, value_acc), query_grad)

    zero_rows = jnp.zeros((length, local_heads, HD), jnp.float32)
    (key_grad, value_grad), query_blocks = lax.scan(
        attend_back, (zero_rows, zero_rows), (block_starts, lse_blocks)
    )
    query_grad = query_blocks.reshape(length, local_heads, HD)

    def turn(field_in):
        return rotate(field_in, cosine, sines)

    turn_back = jax.vjp(turn, zero_rows)[1]
    projected_grad = jnp.stack(
        [turn_back(query_grad)[0], turn_back(key_grad)[0], value_grad], axis=1
    )
    projected_grad = projected_grad.astype(jnp.bfloat16).reshape(length, 3 * head_cols)
    qkv_weight_grad = jnp.einsum(
        "ld,lc->dc", attn_full, projected_grad, preferred_element_type=jnp.float32
    )
    qkv_weight_grad = qkv_weight_grad.reshape(model_width, 3, head_cols)
    qkv_bias_grad = jnp.sum(projected_grad, axis=0, dtype=jnp.float32).reshape(3, head_cols)
    attn_in_grad = jnp.einsum(
        "lc,dc->ld",
        projected_grad,
        full_qkv.reshape(model_width, 3 * head_cols),
        preferred_element_type=jnp.float32,
    )
    reduced = (
        lax.psum_scatter(qkv_weight_grad, "dp", scatter_dimension=0, tiled=True),
        lax.psum_scatter(qkv_bias_grad, "dp", scatter_dimension=1, tiled=True),
        lax.psum_scatter(dense_grad, "dp", scatter_dimension=0, tiled=True),
        lax.psum_scatter(up_grad, "dp", scatter_dimension=0, tiled=True),
        lax.psum_scatter(up_bias_grad, "dp", scatter_dimension=0, tiled=True),
        lax.psum_scatter(down_grad, "dp", scatter_dimension=0, tiled=True),
    )
    attn_local, mlp_local = (
        lax.psum_scatter(
            attn_in_grad.astype(jnp.bfloat16), "tensor", scatter_dimension=0, tiled=True
        ).astype(jnp.float32),
        lax.psum_scatter(
            mlp_in_grad.astype(jnp.bfloat16), "tensor", scatter_dimension=0, tiled=True
        ).astype(jnp.float32),
    )
    pull_attn = jax.vjp(layer_norm, own_rows, small_vecs[0], small_vecs[1])[1]
    pull_mlp = jax.vjp(layer_norm, own_rows, small_vecs[2], small_vecs[3])[1]
    rows_grad_attn, gain_grad_attn, shift_grad_attn = pull_attn(attn_local)
    rows_grad_mlp, gain_grad_mlp, shift_grad_mlp = pull_mlp(mlp_local)
    cot_rows = out_grad.astype(jnp.float32)
    input_grad = (cot_rows + rows_grad_attn + rows_grad_mlp).astype(jnp.bfloat16)
    bias_total = jnp.sum(cot_rows, axis=0)
    small_sums = (
        lax.psum_scatter(gain_grad_attn, ("dp", "tensor"), scatter_dimension=0, tiled=True),
        lax.psum_scatter(shift_grad_attn, ("dp", "tensor"), scatter_dimension=0, tiled=True),
        lax.psum_scatter(gain_grad_mlp, ("dp", "tensor"), scatter_dimension=0, tiled=True),
        lax.psum_scatter(shift_grad_mlp, ("dp", "tensor"), scatter_dimension=0, tiled=True),
        lax.psum_scatter(bias_total, ("dp", "tensor"), scatter_dimension=0, tiled=True),
    )
    return (
        layer_out,
        input_grad,
        small_sums[0],
        small_sums[1],
        small_sums[2],
        small_sums[3],
        reduced[0],
        reduced[1],
        reduced[2],
        small_sums[4],
        reduced[3],
        reduced[4],
        reduced[5],
        small_sums[4],
    )


def solution(mesh):
    in_specs = (
        P(("dp", "tensor"), None),
        P(("dp", "tensor"), None),
        P("dp", None),
        P("dp", None),
        P(("dp", "tensor")),
        P(("dp", "tensor")),
        P(("dp", "tensor")),
        P(("dp", "tensor")),
        P("dp", None, "tensor"),
        P(None, ("tensor", "dp")),
        P(("tensor", "dp"), None),
        P(("dp", "tensor")),
        P("dp", "tensor"),
        P(("tensor", "dp")),
        P(("tensor", "dp"), None),
        P(("dp", "tensor")),
    )
    out_specs = (
        P(("dp", "tensor"), None),
        P(("dp", "tensor"), None),
        P(("dp", "tensor")),
        P(("dp", "tensor")),
        P(("dp", "tensor")),
        P(("dp", "tensor")),
        P("dp", None, "tensor"),
        P(None, ("tensor", "dp")),
        P(("tensor", "dp"), None),
        P(("dp", "tensor")),
        P("dp", "tensor"),
        P(("tensor", "dp")),
        P(("tensor", "dp"), None),
        P(("dp", "tensor")),
    )
    return jax.shard_map(shards, mesh=mesh, in_specs=in_specs, out_specs=out_specs, check_vma=False)
```

profile of v0, /device:TPU:0, one launch (start us, length us, event | category | flops | bytes accessed | tf_op | source)
XLA Modules:
  0.0 704.2 jit_solution(13958768486302023803)
XLA Ops:
  15.1 42.2 %all-reduce.21 = (bf16[1024]{0:T(1024)(128)(2,1)S(1)}, bf16[1024]{0:T(1024)(128)(2,1)S(1)}, bf16[1024]{0:T(1024)(128)(2,1)S(1)}, bf16[1024]{0:T(1024)(128)(2,1)S...) all-reduce(bf16[1024]{0:T(1024)(128)(2,1)S(1)} %dynamic-update-slic, ...), channel_id=1, replica_groups=mesh['dp'=16,'tensor'=2] {'dp','tensor'}, use_global_device_ids=true, to_apply=%add.11 | all-reduce | flops 6144 | bytes 24576
  57.3 21.3 %all-gather = bf16[16,32,3]{1,2,0:T(4,128)(2,1)S(1)} all-gather(bf16[1,32,3]{1,2,0:T(4,128)(2,1)} %bitcast.96), channel_id=1, replica_groups=mesh['dp'=16,'tensor'=2] {'dp'}, dimensions={0}, use_global_device_ids=true | all-gather | bytes 3264 | tf_op jit(solution)/shard_map/all_gather | solution.py:82
  78.7 17.6 %all-gather.1 = bf16[16,1,128]{2,1,0:T(2,128)(2,1)S(1)} all-gather(bf16[1,1,128]{2,1,0:T(2,128)(2,1)} %bitcast.97), channel_id=1, replica_groups=mesh['dp'=16,'tensor'=2] {'dp'}, dimensions={0}, use_global_device_ids=true | all-gather | bytes 4352 | tf_op jit(solution)/shard_map/all_gather | solution.py:85
  101.4 9.2 %all_gather.51 = bf16[256,1024]{1,0:T(8,128)(2,1)S(1)} all-gather(bf16[128,1024]{1,0:T(8,128)(2,1)S(1)} %get-tuple-element.105), channel_id=1, replica_groups=mesh['dp'=16,'tensor'=2] {'tensor'}, dimensions={0}, use_global_device_ids=true | all-gather | bytes 786432 | tf_op jit(solution)/shard_map/all_gather | solution.py:77
  110.6 8.5 %all_gather.63 = bf16[256,1024]{1,0:T(8,128)(2,1)S(1)} all-gather(bf16[128,1024]{1,0:T(8,128)(2,1)S(1)} %copy-done.9), channel_id=1, replica_groups=mesh['dp'=16,'tensor'=2] {'tensor'}, dimensions={0}, use_global_device_ids=true | all-gather | bytes 786432 | tf_op jit(solution)/shard_map/all_gather | solution.py:147
  119.0 7.7 %all_gather.57 = bf16[256,1024]{1,0:T(8,128)(2,1)} all-gather(bf16[128,1024]{1,0:T(8,128)(2,1)S(1)} %get-tuple-element.106), channel_id=1, replica_groups=mesh['dp'=16,'tensor'=2] {'tensor'}, dimensions={0}, use_global_device_ids=true | all-gather | bytes 786432 | tf_op jit(solution)/shard_map/all_gather | solution.py:78
  126.9 1.7 convolution_convert_fusion.4
  129.4 4.7 copy.67
  134.1 4.1 convolution_add_fusion
  138.2 1.9 copy.69
  142.3 1.6 multiply_reduce_fusion
  147.0 3.8 convolution_convert_fusion.2
  151.1 5.0 convolution_add_fusion.1
  156.1 44.1 %all-gather.13.cloned.1.call-done = bf16[2048,1024]{1,0:T(8,128)(2,1)} async-done(((bf16[128,1024]{1,0:T(8,128)(2,1)}), bf16[2048,1024]{1,0:T(8,128)(2,1)}) %all-gather.13.cloned.1.call-update) | async-done | bytes 4194320 | tf_op jit(solution)/shard_map/all_gather | solution.py:86
  200.2 9.0 %convert_reduce_fusion = (f32[2048]{0:T(1024)S(1)}, bf16[256,2048]{1,0:T(8,128)(2,1)S(1)}, f32[256,2048]{1,0:T(8,128)}) fusion(f32[256,2048]{1,0:T(8,128)} %convolution_add_fusion.1, bf16[256,1024]{1,0:T(8,128)(2,1)S(1)} %all_gather.63, bf16[2048,1024]{1,0:T(8,128)(2,1)} %all-gather.13.cloned.1.call-done), kind=kOutput, calls=%fused_computation.4 | convolution fusion | flops 1112537088 | bytes 9969664 | tf_op jit(solution)/shard_map/ld,fd->lf/dot_general | solution.py:156
  210.2 2.1 convolution_convert_fusion.1
  216.0 2.8 multiply_convert_fusion.1
  219.6 2.1 convolution_convert_fusion.3
  221.8 1.8 fusion.58
  223.6 3.7 fusion.36
  227.4 4.5 fusion.60
  233.3 4.5 fusion.59
  239.7 18.3 %reduce-scatter.28.cloned.1.call-done = f32[32,3]{1,0:T(8,128)} async-done(((f32[512,3]{1,0:T(8,128)}), f32[32,3]{1,0:T(8,128)}) %reduce-scatter.28.cloned.1.call-update) | async-done | bytes 400
  259.3 30.2 %all-reduce.19 = f32[2048]{0:T(1024)S(1)} all-reduce(f32[2048]{0:T(1024)S(1)} %get-tuple-element.92), channel_id=15, replica_groups=mesh['dp'=16,'tensor'=2] {'dp'}, use_global_device_ids=true, to_apply=%region_30.31.clone | all-reduce | flops 2048 | bytes 16384
  293.6 13.8 %reduce-scatter.12.cloned.1.call-done = bf16[128,1024]{1,0:T(8,128)(2,1)} async-done(((bf16[256,1024]{1,0:T(8,128)(2,1)}), bf16[128,1024]{1,0:T(8,128)(2,1)}) %reduce-scatter.12.cloned.1.call-update) | async-done | bytes 262160 | tf_op jit(solution)/shard_map/reduce_scatter | solution.py:135
  307.4 16.9 %reduce-scatter.14.cloned.1.call-done = bf16[128,1024]{1,0:T(8,128)(2,1)} async-done(((bf16[256,1024]{1,0:T(8,128)(2,1)}), bf16[128,1024]{1,0:T(8,128)(2,1)}) %reduce-scatter.14.cloned.1.call-update) | async-done | bytes 262160 | tf_op jit(solution)/shard_map/reduce_scatter | solution.py:143
  324.3 2.4 convert_reduce_fusion.5
  326.8 39.8 %all-reduce.20 = (f32[1024]{0:T(1024)S(1)}, f32[1024]{0:T(1024)S(1)}, f32[1024]{0:T(1024)S(1)}, f32[1024]{0:T(1024)S(1)}, f32[1024]{0:T(1024)S(1)}) all-reduce(f32[1024]{0:T(1024)S(1)} %get-tuple-element.76, f32[1024]{0:T(1024)S(1)} %get-tuple-element.80, ...), channel_id=6, replica_groups=mesh['dp'=16,'tensor'=2] {'dp','tensor'}, use_global_device_ids=true, to_apply=%region_15.16.clone | all-reduce | flops 5120 | bytes 40960
  368.9 21.7 %reduce-scatter.22.cloned.1.call-done = f32[32,1024]{1,0:T(8,128)} async-done(((f32[512,1024]{1,0:T(8,128)}), f32[32,1024]{1,0:T(8,128)}) %reduce-scatter.22.cloned.1.call-update) | async-done | bytes 131088 | tf_op jit(solution)/shard_map/reduce_scatter | solution.py:219
  390.7 89.3 %reduce-scatter.20.cloned.1.call-done = f32[64,3,512]{2,0,1:T(8,128)} async-done(((f32[1024,3,512]{2,0,1:T(8,128)}), f32[64,3,512]{2,0,1:T(8,128)}) %reduce-scatter.20.cloned.1.call-update) | async-done | bytes 393232 | tf_op jit(solution)/shard_map/reduce_scatter | solution.py:217
  479.9 108.2 %reduce-scatter.26.cloned.1.call-done = f32[128,1024]{1,0:T(8,128)} async-done(((f32[2048,1024]{1,0:T(8,128)}), f32[128,1024]{1,0:T(8,128)}) %reduce-scatter.26.cloned.1.call-update) | async-done | bytes 524304 | tf_op jit(solution)/shard_map/reduce_scatter | solution.py:222
  588.1 109.0 %reduce-scatter.24.cloned.1.call-done = f32[64,2048]{1,0:T(8,128)} async-done(((f32[1024,2048]{1,0:T(8,128)}), f32[64,2048]{1,0:T(8,128)}) %reduce-scatter.24.cloned.1.call-update) | async-done | bytes 524304 | tf_op jit(solution)/shard_map/reduce_scatter | solution.py:220
  (139 shorter events, 35.8 us)
Async XLA Ops:
  7.2 103.4 %copy-start.9 = (bf16[128,1024]{1,0:T(8,128)(2,1)S(1)}, bf16[128,1024]{1,0:T(8,128)(2,1)}, u32[]{:S(2)}) copy-start(bf16[128,1024]{1,0:T(8,128)(2,1)} %param.17) | copy-start | bytes 786436
  7.2 119.7 %all-gather.9.cloned.1.call-start = ((), (), s32[]{:S(2)}) async-start(), calls=%async_computation.10 | async-start | bytes 1114112 | tf_op jit(solution)/shard_map/all_gather | solution.py:83
  7.9 121.5 %all-gather.7.cloned.1.call-start = ((), (), s32[]{:S(2)}) async-start(), calls=%async_computation.9 | async-start | bytes 3342336 | tf_op jit(solution)/shard_map/all_gather | solution.py:81
  8.7 142.4 %all-gather.11.cloned.1.call-start = ((), (), s32[]{:S(2)}) async-start(), calls=%async_computation.12 | async-start | bytes 4456448 | tf_op jit(solution)/shard_map/all_gather | solution.py:84
  9.4 190.8 %all-gather.13.cloned.1.call-start = ((), (), s32[]{:S(2)}) async-start(), calls=%async_computation.13 | async-start | bytes 4456448 | tf_op jit(solution)/shard_map/all_gather | solution.py:86
  10.0 248.0 %reduce-scatter.28.cloned.1.call-start = ((), (), s32[]{:S(2)}) async-start(), calls=%async_computation.21 | async-start | bytes 278528
  110.6 23.6 %copy-start.5 = (bf16[256,1024]{1,0:T(8,128)(2,1)}, bf16[256,1024]{1,0:T(8,128)(2,1)S(1)}, u32[]{:S(2)}) copy-start(bf16[256,1024]{1,0:T(8,128)(2,1)S(1)} %all_gather.51) | copy-start | bytes 1572868
  140.1 1.2 copy-start.1
  141.3 1.0 copy-start.3
  147.0 143.2 %reduce-scatter.16.cloned.1.call-start = ((), (), s32[]{:S(2)}) async-start(), calls=%async_computation.15 | async-start | bytes 786432 | tf_op jit(solution)/shard_map/reduce_scatter | solution.py:225
  150.9 139.8 %reduce-scatter.18.cloned.1.call-start = ((), (), s32[]{:S(2)}) async-start(), calls=%async_computation.16 | async-start | bytes 786432 | tf_op jit(solution)/shard_map/reduce_scatter | solution.py:228
  200.2 10.0 %copy-start.14 = (bf16[1024,2048]{1,0:T(8,128)(2,1)S(1)}, bf16[1024,2048]{1,0:T(8,128)(2,1)}, u32[]{:S(2)}) copy-start(bf16[1024,2048]{1,0:T(8,128)(2,1)} %all-gather.11.cloned.1.call-done) | copy-start | bytes 12582916
  209.2 1.0 copy-start.7
  212.3 95.1 %reduce-scatter.12.cloned.1.call-start = ((), (), s32[]{:S(2)}) async-start(), calls=%async_computation.11 | async-start | bytes 786432 | tf_op jit(solution)/shard_map/reduce_scatter | solution.py:135
  212.4 2.3 copy-start.2
  214.0 0.7 copy-start.11
  216.0 108.3 %reduce-scatter.14.cloned.1.call-start = ((), (), s32[]{:S(2)}) async-start(), calls=%async_computation.14 | async-start | bytes 786432 | tf_op jit(solution)/shard_map/reduce_scatter | solution.py:143
  216.0 3.5 copy-start.13
  219.6 2.2 copy-start.12
  221.7 1.9 copy-start.6
  221.7 169.0 %reduce-scatter.22.cloned.1.call-start = ((), (), s32[]{:S(2)}) async-start(), calls=%async_computation.18 | async-start | bytes 2228224 | tf_op jit(solution)/shard_map/reduce_scatter | solution.py:219
  223.6 256.4 %reduce-scatter.20.cloned.1.call-start = ((), (), s32[]{:S(2)}) async-start(), calls=%async_computation.17 | async-start | bytes 6684672 | tf_op jit(solution)/shard_map/reduce_scatter | solution.py:217
  227.4 360.8 %reduce-scatter.26.cloned.1.call-start = ((), (), s32[]{:S(2)}) async-start(), calls=%async_computation.20 | async-start | bytes 8912896 | tf_op jit(solution)/shard_map/reduce_scatter | solution.py:222
  231.9 1.0 copy-start.4
  231.9 1.4 copy-start.8
  232.0 465.2 %reduce-scatter.24.cloned.1.call-start = ((), (), s32[]{:S(2)}) async-start(), calls=%async_computation.19 | async-start | bytes 8912896 | tf_op jit(solution)/shard_map/reduce_scatter | solution.py:220
  237.8 0.7 copy-start.15
  237.8 52.8 %copy-start = (bf16[128,1024]{1,0:T(8,128)(2,1)S(1)}, bf16[128,1024]{1,0:T(8,128)(2,1)}, u32[]{:S(2)}) copy-start(bf16[128,1024]{1,0:T(8,128)(2,1)} %param.16) | copy-start | bytes 786436
  237.8 86.5 %copy-start.10 = (bf16[128,1024]{1,0:T(8,128)(2,1)S(1)}, bf16[128,1024]{1,0:T(8,128)(2,1)}, u32[]{:S(2)}) copy-start(bf16[128,1024]{1,0:T(8,128)(2,1)} %param.17) | copy-start | bytes 786436
  366.6 331.0 %copy-start.16 = (f32[32]{0:T(128)}, f32[32]{0:T(128)S(1)}, u32[]{:S(2)}) copy-start(f32[32]{0:T(128)S(1)} %dynamic-slice.4) | copy-start | bytes 388
Sparse Core Ops, SparseCore 0:
  10.2 40.7 all-gather.8
  53.1 44.3 all-gather.6
  99.7 49.3 all-gather.10
  151.1 49.0 all-gather.12
  204.1 53.7 reduce-scatter.27
  260.1 13.5 reduce-scatter.15
  276.0 14.5 reduce-scatter.17
  292.9 14.5 reduce-scatter.11
  309.8 14.5 reduce-scatter.13
  328.5 62.1 reduce-scatter.21
  395.7 84.1 reduce-scatter.19
  484.4 103.6 reduce-scatter.25
  592.8 104.3 reduce-scatter.23
where the time goes:
time: 705 us; the launch traced here: 704 us
  waiting for transfers between devices  425 us (60%)
  blocking collectives  176 us (25%)
  matrix products  48.5 us (7%)
  local copies, waits for them, and re-layouts  24.5 us (3%)
  between operations  15 us (2%)
  other arithmetic  14.6 us (2%)
    unnamed x3, blocking collectives  112 us
    reduce_scatter x1, waiting for transfers between devices, shards(): lax.psum_scatter(up_grad, 'dp', scatter_dimension=0, tiled=True)  109 us
    reduce_scatter x1, waiting for transfers between devices, shards(): lax.psum_scatter(down_grad, 'dp', scatter_dimension=0, tiled=True)  108 us
    reduce_scatter x1, waiting for transfers between devices, shards(): lax.psum_scatter(qkv_weight_grad, 'dp', scatter_dimension=0, tiled=True)  89.3 us
    all_gather x1, waiting for transfers between devices, shards(): lax.all_gather(down_weight, 'dp', axis=0, tiled=True)  44.1 us
    reduce_scatter x1, waiting for transfers between devices, shards(): lax.psum_scatter(dense_grad, 'dp', scatter_dimension=0, tiled=True)  21.7 us
    all_gather x1, blocking collectives, shards(): lax.all_gather(qkv_bias, 'dp', axis=1, tiled=True)  21.3 us
    unnamed x14, waiting for transfers between devices  21 us
  transfers between devices with their start and end apart: 13, of which 9 were waited for; matrix products, arithmetic and copies ran while one was open for 12% of the time, Pallas kernels for 0%

commit v1 on v0

--- a/solution.py
+++ b/solution.py
@@ -1,6 +1,9 @@
 import jax
 import jax.numpy as jnp
+import numpy as np
 from jax import lax
+from jax.experimental import pallas as pl
+from jax.experimental.pallas import tpu as pltpu
 from jax.sharding import PartitionSpec as P
 
 HD = 64
@@ -261,6 +264,1076 @@
     )
 
 
+F32 = jnp.float32
+BF16 = jnp.bfloat16
+MESH_ID = pl.DeviceIdType.MESH
+LINE = 4
+SEQ = 256
+WIDTH = 1024
+HID = 512
+PAIR = 128
+
+
+def nn(a, b):
+    return jnp.dot(a, b, preferred_element_type=F32)
+
+
+def nt(a, b):
+    return lax.dot_general(a, b, (((1,), (1,)), ((), ())), preferred_element_type=F32)
+
+
+def tn(a, b):
+    return lax.dot_general(a, b, (((0,), (0,)), ((), ())), preferred_element_type=F32)
+
+
+def turn_tables():
+    position = np.arange(SEQ, dtype=np.float64)[:, None]
+    lane = np.arange(PAIR) % HD
+    rates = 10000.0 ** (-(lane % (ROT // 2)) * (2.0 / ROT))
+    angles = position * rates[None, :]
+    cosine = np.where(lane < ROT, np.cos(angles), 1.0)
+    toward = np.where(lane < ROT // 2, -np.sin(angles), 0.0)
+    away = np.where((lane >= ROT // 2) & (lane < ROT), np.sin(angles), 0.0)
+    return np.stack([cosine, toward, away]).astype(np.float32)
+
+
+def rows_of(index, count):
+    return pl.ds(pl.multiple_of(index * count, count), count)
+
+
+class Place:
+    def __init__(self):
+        index = lax.axis_index("dp")
+        self.t = lax.axis_index("tensor")
+        self.z = index // 4
+        self.k = index % 4
+        self.y = self.k // 2
+        self.c = self.k % 2
+        self.kc = self.y * 2 + 1 - self.c
+        self.ky = (1 - self.y) * 2 + self.c
+        self.kyc = (1 - self.y) * 2 + 1 - self.c
+        self.q = self.k * 2 + self.t
+        self.core = self.at(self.z, self.kc, self.t)
+        self.cross = (
+            self.at(self.z, self.k, 1 - self.t),
+            self.at(self.z, self.ky, self.t),
+            self.at(self.z, self.ky, 1 - self.t),
+        )
+
+    def at(self, z, k, t):
+        return (z * 4 + k, t)
+
+    def line(self, z):
+        return self.at(z, self.k, self.t)
+
+
+class Wires:
+    def __init__(self, sends, arrivals):
+        self.sends, self.arrivals, self.used = sends, arrivals, 0
+
+    def take(self, count):
+        first = self.used
+        self.used += count
+        return first
+
+    def copy(self, slot, src, dst, device):
+        return pltpu.make_async_remote_copy(
+            src_ref=src,
+            dst_ref=dst,
+            send_sem=self.sends.at[slot],
+            recv_sem=self.arrivals.at[slot],
+            device_id=device,
+            device_id_type=MESH_ID,
+        )
+
+
+class PlaneGather:
+    def __init__(self, me, wires, src, slot):
+        self.me, self.wires, self.src, self.slot = me, wires, src, slot
+        self.first = wires.take(7)
+        self.from_cross = (me.k * 2 + 1 - me.t, me.ky * 2 + me.t, me.ky * 2 + 1 - me.t)
+        self.from_core = (
+            me.kc * 2 + me.t,
+            me.kc * 2 + 1 - me.t,
+            me.kyc * 2 + me.t,
+            me.kyc * 2 + 1 - me.t,
+        )
+
+    def near(self, which, block):
+        return self.wires.copy(
+            self.first + which, self.slot(block), self.slot(block), self.me.core
+        )
+
+    def far(self, which, block):
+        src = self.src if block is None else self.slot(block)
+        dst = self.slot(self.me.q if block is None else block)
+        return self.wires.copy(self.first + 4 + which, src, dst, self.me.cross[which])
+
+    def own(self):
+        return self.wires.copy(self.first, self.src, self.slot(self.me.q), self.me.core)
+
+    def start(self):
+        for which in range(3):
+            self.far(which, None).start()
+        self.own().start()
+
+    def forward(self):
+        for which in range(3):
+            self.far(which, self.from_cross[which]).wait_recv()
+            self.near(1 + which, self.from_cross[which]).start()
+
+    def finish(self):
+        for which in range(4):
+            self.near(which, self.from_core[which]).wait_recv()
+
+    def drain(self):
+        self.own().wait_send()
+        for which in range(3):
+            self.far(which, None).wait_send()
+            self.near(1 + which, self.from_cross[which]).wait_send()
+
+
+class LineGather:
+    def __init__(self, me, wires, views):
+        self.me, self.wires, self.views = me, wires, views
+        self.first = wires.take(6 * len(views))
+
+    def part(self, way, hop, which, block):
+        z = self.me.z
+        view = self.views[which](block)
+        slot = self.first + (way * 3 + hop) * len(self.views) + which
+        return self.wires.copy(slot, view, view, self.me.line(z + 1 if way == 0 else z - 1))
+
+    def each(self, way, hop, block, act):
+        for which in range(len(self.views)):
+            act(self.part(way, hop, which, block))
+
+    def send(self, hop, act):
+        z = self.me.z
+
+        @pl.when((z >= hop) & (z < LINE - 1))
+        def _():
+            self.each(0, hop, z - hop, act)
+
+        @pl.when((z + hop < LINE) & (z > 0))
+        def _():
+            self.each(1, hop, z + hop, act)
+
+    def arrive(self, hop):
+        z = self.me.z
+
+        @pl.when(z > hop)
+        def _():
+            self.each(0, hop, z - 1 - hop, lambda copy: copy.wait_recv())
+
+        @pl.when(z + 1 + hop < LINE)
+        def _():
+            self.each(1, hop, z + 1 + hop, lambda copy: copy.wait_recv())
+
+    def start(self):
+        self.send(0, lambda copy: copy.start())
+
+    def relay(self, hop):
+        self.arrive(hop - 1)
+        self.send(hop, lambda copy: copy.start())
+
+    def finish(self):
+        self.arrive(LINE - 2)
+
+    def drain(self):
+        for hop in range(LINE - 1):
+            self.send(hop, lambda copy: copy.wait_send())
+
+
+class LineReduce:
+    def __init__(self, me, wires, held, landed):
+        self.me, self.wires, self.held, self.landed = me, wires, held, landed
+        self.first = wires.take(2 * LINE)
+
+    def copy(self, way, block):
+        z = self.me.z
+        device = self.me.line(z - 1 if way == 0 else z + 1)
+        return self.wires.copy(
+            self.first + way * LINE + block, self.held(block), self.landed(way, block), device
+        )
+
+    def join(self, way, block):
+        self.copy(way, block).wait_recv()
+        total = self.held(block)[...].astype(F32) + self.landed(way, block)[...].astype(F32)
+        self.held(block)[...] = total.astype(BF16)
+
+    def step(self, index):
+        z = self.me.z
+        low, high = index, LINE - 1 - index
+
+        @pl.when(z > low)
+        def _():
+            @pl.when(z < LINE - 1)
+            def _():
+                self.join(0, low)
+
+            self.copy(0, low).start()
+
+        @pl.when(z < high)
+        def _():
+            @pl.when(z > 0)
+            def _():
+                self.join(1, high)
+
+            self.copy(1, high).start()
+
+    def finish(self):
+        z = self.me.z
+
+        @pl.when(z < LINE - 1)
+        def _():
+            self.join(0, z)
+
+        @pl.when(z > 0)
+        def _():
+            self.join(1, z)
+
+    def drain(self):
+        z = self.me.z
+        for index in range(LINE - 1):
+
+            @pl.when(z > index)
+            def _():
+                self.copy(0, index).wait_send()
+
+            @pl.when(z < LINE - 1 - index)
+            def _():
+                self.copy(1, LINE - 1 - index).wait_send()
+
+
+class PlaneReduce:
+    def __init__(self, me, wires, part, paired, crossed):
+        self.me, self.wires = me, wires
+        self.part, self.paired, self.crossed = part, paired, crossed
+        self.first = wires.take(5)
+        self.blocks = (me.k * 2 + 1 - me.t, me.ky * 2 + me.t, me.ky * 2 + 1 - me.t)
+
+    def pair(self, y):
+        rows = rows_of(y * 2 + 1 - self.me.c, SEQ)
+        return self.wires.copy(
+            self.first + y, self.part.at[rows], self.paired.at[y], self.me.core
+        )
+
+    def start(self):
+        for y in range(2):
+            self.pair(y).start()
+
+    def cross(self, which):
+        return self.wires.copy(
+            self.first + 2 + which,
+            self.part.at[rows_of(self.blocks[which], 128)],
+            self.crossed.at[which],
+            self.me.cross[which],
+        )
+
+    def middle(self):
+        for y in range(2):
+            self.pair(y).wait_recv()
+            rows = rows_of(y * 2 + self.me.c, SEQ)
+            total = self.part[rows].astype(F32) + self.paired[y].astype(F32)
+            self.part[rows] = total.astype(BF16)
+        for which in range(3):
+            self.cross(which).start()
+
+    def finish(self):
+        for which in range(3):
+            self.cross(which).wait_recv()
+        total = self.part[rows_of(self.me.q, 128)].astype(F32)
+        for which in range(3):
+            total = total + self.crossed[which].astype(F32)
+        return total
+
+    def drain(self):
+        for y in range(2):
+            self.pair(y).wait_send()
+        for which in range(3):
+            self.cross(which).wait_send()
+
+
+def layer_kernel(
+    x_hbm,
+    g_hbm,
+    small_hbm,
+    qkv_hbm,
+    dense_hbm,
+    up_hbm,
+    down_hbm,
+    turn_ref,
+    layer_out_ref,
+    input_grad_ref,
+    qkv_grad_ref,
+    dense_grad_ref,
+    up_grad_ref,
+    down_grad_ref,
+    small_out_ref,
+    x_all,
+    g_all,
+    small_line,
+    small_all,
+    qkv_w,
+    dense_w,
+    up_w,
+    down_w,
+    vec_ref,
+    bias_ref,
+    normed_a,
+    normed_m,
+    context_ref,
+    turned_grad,
+    active_ref,
+    hidden_grad,
+    part_out,
+    part_attn,
+    part_mlp,
+    paired_ref,
+    crossed_ref,
+    up_held,
+    up_landed,
+    down_held,
+    down_landed,
+    qkv_held,
+    qkv_landed,
+    up_final,
+    qkv_final,
+    dense_held,
+    dense_final,
+    qkv_bias_held,
+    qkv_bias_final,
+    up_bias_held,
+    up_bias_final,
+    sums_held,
+    sums_core,
+    sums_cross,
+    sums_line,
+    sends,
+    arrivals,
+    local_sems,
+):
+    me = Place()
+    wires = Wires(sends, arrivals)
+    z, k, t = me.z, me.k, me.t
+
+    barrier = pltpu.get_barrier_semaphore()
+
+    def greet(device):
+        pl.semaphore_signal(barrier, inc=1, device_id=device, device_id_type=MESH_ID)
+
+    greet(me.core)
+    greet(me.at(z, me.kyc, t))
+    for device in me.cross:
+        greet(device)
+    for step in range(1, LINE):
+        greet(me.line((z + step) % LINE))
+    for other in range(4):
+
+        @pl.when((k != z) | (z != other))
+        def _():
+            greet(me.at(other, z, t))
+
+        @pl.when((k != z) | (k != other))
+        def _():
+            greet(me.at(k, other, t))
+
+    pl.semaphore_wait(barrier, jnp.where(k == z, 14, 16))
+
+    local_copies = []
+
+    def local(src, dst):
+        copy = pltpu.make_async_copy(src, dst, local_sems.at[len(local_copies)])
+        local_copies.append(copy)
+        copy.start()
+
+    seat = pl.ds(pl.multiple_of(z * 256 + k * 64, 64), 64)
+    local(qkv_hbm.at[:, :, rows_of(k, PAIR)], qkv_w.at[:, seat, :])
+    local(x_hbm, x_all.at[rows_of(me.q, 128)])
+    local(g_hbm, g_all.at[rows_of(me.q, 128)])
+    for other in range(LINE):
+        local(
+            up_hbm.at[:, rows_of(other * 4 + k, 128)],
+            up_w.at[seat, pl.ds(other * 128, 128)],
+        )
+    local(down_hbm, down_w.at[rows_of(z, 128)])
+    local(small_hbm, small_line.at[z])
+
+    first_small = wires.take(3)
+
+    def small_copy(step, origin):
+        return wires.copy(
+            first_small + step - 1,
+            small_hbm,
+            small_line.at[origin],
+            me.line((z + step) % LINE),
+        )
+
+    for step in range(1, LINE):
+        small_copy(step, z).start()
+
+    peers = (me.kc, me.ky, me.kyc)
+    first_qkv = wires.take(3)
+
+    def qkv_copy(which, origin):
+        peer = peers[which]
+        place = pl.ds(pl.multiple_of(z * 256 + origin * 64, 64), 64)
+        return wires.copy(
+            first_qkv + which,
+            qkv_hbm.at[:, :, rows_of(peer, PAIR)],
+            qkv_w.at[:, place, :],
+            me.at(z, peer, t),
+        )
+
+    for which in range(3):
+        qkv_copy(which, k).start()
+
+    gather_x = PlaneGather(me, wires, x_hbm, lambda block: x_all.at[rows_of(block, 128)])
+    gather_x.start()
+
+    first_dense = wires.take(4)
+
+    def dense_copy(other):
+        return wires.copy(
+            first_dense + k, dense_hbm, dense_w.at[rows_of(k, 32)], me.at(other, z, t)
+        )
+
+    first_dense_send = wires.take(4)
+
+    def dense_send(other):
+        return pltpu.make_async_remote_copy(
+            src_ref=dense_hbm,
+            dst_ref=dense_w.at[rows_of(k, 32)],
+            send_sem=sends.at[first_dense_send + other],
+            recv_sem=arrivals.at[first_dense + k],
+            device_id=me.at(other, z, t),
+            device_id_type=MESH_ID,
+        )
+
+    def dense_arrival(other):
+        return wires.copy(
+            first_dense + other, dense_hbm, dense_w.at[rows_of(other, 32)], me.at(k, other, t)
+        )
+
+    own_dense = pltpu.make_async_copy(
+        dense_hbm, dense_w.at[rows_of(k, 32)], local_sems.at[len(local_copies)]
+    )
+    for other in range(4):
+
+        @pl.when((k != z) | (z != other))
+        def _():
+            dense_send(other).start()
+
+        @pl.when((k == z) & (z == other))
+        def _():
+            own_dense.start()
+
+    first_up = wires.take(12)
+
+    def up_copy(which, other, origin):
+        peer = peers[which]
+        place = pl.ds(pl.multiple_of(z * 256 + origin * 64, 64), 64)
+        return wires.copy(
+            first_up + which * 4 + other,
+            up_hbm.at[:, rows_of(other * 4 + peer, 128)],
+            up_w.at[place, pl.ds(other * 128, 128)],
+            me.at(z, peer, t),
+        )
+
+    for which in range(3):
+        for other in range(LINE):
+            up_copy(which, other, k).start()
+
+    gather_g = PlaneGather(me, wires, g_hbm, lambda block: g_all.at[rows_of(block, 128)])
+    gather_g.start()
+
+    for copy in local_copies:
+        copy.wait()
+
+    for which in range(3):
+        qkv_copy(which, peers[which]).wait_recv()
+    line_qkv = LineGather(me, wires, [lambda s: qkv_w.at[:, rows_of(s, 256), :]])
+    line_qkv.start()
+    for which in range(3):
+        for other in range(LINE):
+            up_copy(which, other, peers[which]).wait_recv()
+    line_mlp = LineGather(
+        me,
+        wires,
+        [lambda s: up_w.at[rows_of(s, 256)], lambda s: down_w.at[rows_of(s, 128)]],
+    )
+    line_mlp.start()
+
+    for step in range(1, LINE):
+        small_copy(step, (z + LINE - step) % LINE).wait_recv()
+    gather_small = PlaneGather(me, wires, small_line, lambda block: small_all.at[block])
+    own_small = pltpu.make_async_copy(
+        small_line, small_all.at[me.q], local_sems.at[len(local_copies) + 1]
+    )
+    own_small.start()
+    gather_small.start()
+    gather_x.forward()
+    gather_small.forward()
+    gather_x.finish()
+    gather_small.finish()
+    own_small.wait()
+
+    table = small_all[...].reshape(256, 128).astype(BF16)
+    line_id = lax.broadcasted_iota(jnp.int32, (256, WIDTH), 0)
+    column = lax.broadcasted_iota(jnp.int32, (256, WIDTH), 1)
+    owner = ((line_id >> 3) & 3) * 8 + (line_id >> 5)
+    lane_row = lax.broadcasted_iota(jnp.int32, (128, WIDTH), 0)
+    lane_col = lax.broadcasted_iota(jnp.int32, (128, WIDTH), 1) & 31
+    for kind, count, base in ((0, 4, 0), (1, 2, 4)):
+        chosen = (owner == (column >> 5)) & ((line_id & 7) == kind)
+        spread = tn(table, jnp.where(chosen, 1.0, 0.0).astype(BF16))
+        for which in range(count):
+            picked = jnp.where(lane_row == lane_col + which * 32, spread, 0.0)
+            vec_ref[base + which : base + which + 1, :] = jnp.sum(picked, axis=0, keepdims=True)
+    line_id = line_id[:, :PAIR]
+    column = column[:, :PAIR]
+    chosen = (
+        (((line_id >> 3) & 3) == k)
+        & ((line_id >> 5) == (column >> 5) * 2 + t)
+        & ((line_id & 7) == 2)
+    )
+    spread = tn(table, jnp.where(chosen, 1.0, 0.0).astype(BF16))
+    for which in range(3):
+        picked = jnp.where(lane_row[:, :PAIR] == lane_col[:, :PAIR] + which * 32, spread, 0.0)
+        bias_ref[which : which + 1, :] = jnp.sum(picked, axis=0, keepdims=True)
+
+    def norm_rows(rows):
+        values = x_all[rows].astype(F32)
+        centred = values - jnp.mean(values, axis=-1, keepdims=True)
+        rate = lax.rsqrt(jnp.mean(centred * centred, axis=-1, keepdims=True) + NORM_EPS)
+        return centred * rate, rate
+
+    def norm_block(block, carry):
+        rows = rows_of(block, 128)
+        unit, _ = norm_rows(rows)
+        normed_a[rows] = (unit * vec_ref[0:1, :] + vec_ref[1:2, :]).astype(BF16)
+        normed_m[rows] = (unit * vec_ref[2:3, :] + vec_ref[3:4, :]).astype(BF16)
+        return carry
+
+    lax.fori_loop(0, 8, norm_block, 0)
+
+    gather_g.forward()
+    gather_g.finish()
+    line_qkv.relay(1)
+    line_qkv.relay(2)
+    line_qkv.finish()
+    for other in range(4):
+
+        @pl.when((k != z) | (k != other))
+        def _():
+            dense_arrival(other).wait_recv()
+
+        @pl.when((k == z) & (z == other))
+        def _():
+            own_dense.wait()
+
+    qkv_bias_held[...] = jnp.zeros_like(qkv_bias_held)
+    scale = HD**-0.5
+
+    def attend(seq, carry):
+        rows = rows_of(seq, SEQ)
+        cosine, toward, away = turn_ref[0], turn_ref[1], turn_ref[2]
+        normed = normed_a[rows]
+
+        def project(which):
+            return nn(normed, qkv_w[which]) + bias_ref[which : which + 1, :]
+
+        def turned(field):
+            return (
+                field * cosine
+                + pltpu.roll(field, ROT // 2, 1) * away
+                + pltpu.roll(field, PAIR - ROT // 2, 1) * toward
+            )
+
+        def turned_back(field):
+            return (
+                field * cosine
+                - pltpu.roll(field, ROT // 2, 1) * away
+                - pltpu.roll(field, PAIR - ROT // 2, 1) * toward
+            )
+
+        query = turned(project(0)).astype(BF16)
+        key = turned(project(1)).astype(BF16)
+        value = project(2).astype(BF16)
+        context_grad = nt(g_all[rows], dense_w[...]).astype(BF16)
+
+        spans = small_all[seq * 2, z, 1:2, :]
+        down_pos = lax.broadcasted_iota(jnp.int32, (SEQ, 1), 0).astype(F32)
+        over_pos = lax.broadcasted_iota(jnp.int32, (1, SEQ), 1).astype(F32)
+
+        def labels(place):
+            total = jnp.zeros(place.shape, F32)
+            for span in range(2):
+                begin = spans[:, 64 + span : 65 + span]
+                end = begin + spans[:, 66 + span : 67 + span]
+                total = total + jnp.where((place >= begin) & (place < end), span + 1.0, 0.0)
+            return total
+
+        down_label, over_label = labels(down_pos), labels(over_pos)
+        allowed = (over_pos <= down_pos) | ((down_label == over_label) & (down_label > 0.0))
+
+        lane = lax.broadcasted_iota(jnp.int32, (SEQ, PAIR), 1)
+        parts = []
+        for head in range(2):
+            mine = (lane >= HD) if head else (lane < HD)
+            zero = jnp.zeros_like(query)
+            scores = nt(jnp.where(mine, query, zero), key) * scale
+            scores = jnp.where(allowed, scores, NEG_FILL)
+            exponent = jnp.exp(scores - jnp.max(scores, axis=-1, keepdims=True))
+            probs = exponent * (1.0 / jnp.sum(exponent, axis=-1, keepdims=True))
+            low = probs.astype(BF16)
+            prob_grad = nt(jnp.where(mine, context_grad, zero), value)
+            inner = jnp.sum(prob_grad * probs, axis=-1, keepdims=True)
+            score_grad = (probs * (prob_grad - inner)).astype(BF16)
+            parts.append(
+                (
+                    nn(low, value),
+                    tn(low, context_grad),
+                    nn(score_grad, key) * scale,
+                    tn(score_grad, query) * scale,
+                )
+            )
+        context, value_grad, query_grad, key_grad = (
+            jnp.where(lane < HD, first, second) for first, second in zip(*parts)
+        )
+        context_ref[rows] = context.astype(BF16)
+        grads = (
+            turned_back(query_grad).astype(BF16),
+            turned_back(key_grad).astype(BF16),
+            value_grad.astype(BF16),
+        )
+        total = jnp.zeros((SEQ, WIDTH), F32)
+        for which in range(3):
+            turned_grad[rows, which * PAIR : (which + 1) * PAIR] = grads[which]
+            qkv_bias_held[which : which + 1, :] += jnp.sum(
+                grads[which].astype(F32), axis=0, keepdims=True
+            )
+            total = total + nt(grads[which], qkv_w[which])
+        part_attn[rows] = total.astype(BF16)
+        return carry
+
+    lax.fori_loop(0, 4, attend, 0)
+
+    reduce_attn = PlaneReduce(me, wires, part_attn, paired_ref.at[0], crossed_ref.at[0])
+    reduce_attn.start()
+
+    dense_part = tn(context_ref[...], g_all[...])
+    dense_held[...] = dense_part.astype(BF16)
+
+    def qkv_block(block, carry):
+        grad = tn(normed_a[:, rows_of(block, 256)], turned_grad[...])
+        for which in range(3):
+            qkv_held[block, which] = grad[:, which * PAIR : (which + 1) * PAIR].astype(BF16)
+        return carry
+
+    lax.fori_loop(0, 4, qkv_block, 0)
+
+    first_back = wires.take(8)
+    first_back_send = wires.take(8)
+
+    def back_send(other, kind):
+        src = (dense_held.at[pl.ds(other * 32, 32)], qkv_bias_held)[kind]
+        dst = (dense_final, qkv_bias_final)[kind].at[z]
+        return pltpu.make_async_remote_copy(
+            src_ref=src,
+            dst_ref=dst,
+            send_sem=sends.at[first_back_send + kind * 4 + other],
+            recv_sem=arrivals.at[first_back + kind * 4 + z],
+            device_id=me.at(k, other, t),
+            device_id_type=MESH_ID,
+        )
+
+    def back_arrival(other, kind):
+        src = (dense_held.at[pl.ds(0, 32)], qkv_bias_held)[kind]
+        dst = (dense_final, qkv_bias_final)[kind].at[other]
+        return wires.copy(first_back + kind * 4 + other, src, dst, me.at(other, z, t))
+
+    for other in range(4):
+
+        @pl.when((k != z) | (k != other))
+        def _():
+            back_send(other, 0).start()
+            back_send(other, 1).start()
+
+        @pl.when((k == z) & (k == other))
+        def _():
+            dense_final[z] = dense_held[other * 32 : (other + 1) * 32]
+            qkv_bias_final[z] = qkv_bias_held[...]
+
+    reduce_qkv = LineReduce(
+        me, wires, lambda s: qkv_held.at[s], lambda way, s: qkv_landed.at[way, s]
+    )
+    reduce_attn.middle()
+    for index in range(LINE - 1):
+        reduce_qkv.step(index)
+
+    line_mlp.relay(1)
+    line_mlp.relay(2)
+    line_mlp.finish()
+
+    up_bias_held[...] = jnp.zeros_like(up_bias_held)
+    up_bias = jnp.concatenate([small_all[me.q, s, 3:4, :] for s in range(LINE)], axis=1)
+
+    def feed(tile, carry):
+        rows = rows_of(tile, 128)
+        cotangent = g_all[rows]
+        hidden = nn(normed_m[rows], up_w[...]) + up_bias
+        share = (1.0 + lax.erf(hidden * 0.5**0.5)) * 0.5
+        slope = share + hidden * jnp.exp(hidden * hidden * -0.5) * (2.0 * np.pi) ** -0.5
+        active = (hidden * share).astype(BF16)
+        grad = (nt(cotangent, down_w[...]) * slope).astype(BF16)
+        active_ref[rows] = active
+        hidden_grad[rows] = grad
+        up_bias_held[0:1, :] += jnp.sum(grad.astype(F32), axis=0, keepdims=True)
+        mixed = nn(context_ref[rows], dense_w[...]) + nn(active, down_w[...])
+        part_out[rows] = mixed.astype(BF16)
+        part_mlp[rows] = nt(grad, up_w[...]).astype(BF16)
+        return carry
+
+    lax.fori_loop(0, 8, feed, 0)
+
+    reduce_out = PlaneReduce(me, wires, part_out, paired_ref.at[1], crossed_ref.at[1])
+    reduce_out.start()
+    reduce_mlp = PlaneReduce(me, wires, part_mlp, paired_ref.at[2], crossed_ref.at[2])
+    reduce_mlp.start()
+
+    def down_block(block, carry):
+        down_held[block] = tn(active_ref[:, rows_of(block, 128)], g_all[...]).astype(BF16)
+        return carry
+
+    lax.fori_loop(0, 4, down_block, 0)
+    reduce_down = LineReduce(
+        me, wires, lambda s: down_held.at[s], lambda way, s: down_landed.at[way, s]
+    )
+    reduce_down.step(0)
+
+    def up_block(block, carry):
+        up_held[block] = tn(normed_m[:, rows_of(block, 256)], hidden_grad[...]).astype(BF16)
+        return carry
+
+    lax.fori_loop(0, 4, up_block, 0)
+    reduce_up = LineReduce(
+        me, wires, lambda s: up_held.at[s], lambda way, s: up_landed.at[way, s]
+    )
+    reduce_down.step(1)
+    reduce_up.step(0)
+    reduce_down.step(2)
+    reduce_up.step(1)
+    reduce_up.step(2)
+    reduce_out.middle()
+    reduce_mlp.middle()
+
+    first_ub = wires.take(3)
+
+    def up_bias_copy(step, block, origin):
+        return wires.copy(
+            first_ub + step - 1,
+            up_bias_held.at[:, rows_of(block, 128)],
+            up_bias_final.at[origin],
+            me.line((z + step) % LINE),
+        )
+
+    for step in range(1, LINE):
+        up_bias_copy(step, (z + step) % LINE, z).start()
+    up_bias_final[z] = up_bias_held[:, rows_of(z, 128)]
+
+    reduce_qkv.finish()
+    first_qf = wires.take(3)
+
+    def qkv_out_copy(which, origin):
+        peer = peers[which]
+        return wires.copy(
+            first_qf + which,
+            qkv_held.at[z, :, rows_of(peer, 64), :],
+            qkv_final.at[origin],
+            me.at(z, peer, t),
+        )
+
+    for which in range(3):
+        qkv_out_copy(which, k).start()
+    qkv_final[k] = qkv_held[z, :, rows_of(k, 64), :]
+
+    own = rows_of(me.q, 128)
+    cotangent = g_all[own].astype(F32)
+    mixed = reduce_out.finish()
+    layer_out_ref[...] = (
+        x_all[own].astype(F32) + mixed + vec_ref[4:5, :] + vec_ref[5:6, :]
+    ).astype(BF16)
+    from_attn = reduce_attn.finish()
+    from_mlp = reduce_mlp.finish()
+    unit, rate = norm_rows(own)
+    sums_held[...] = jnp.zeros_like(sums_held)
+    for which, field in enumerate(
+        (from_attn * unit, from_attn, from_mlp * unit, from_mlp, cotangent)
+    ):
+        sums_held[which : which + 1, :] = jnp.sum(field, axis=0, keepdims=True)
+    first_sums = wires.take(7)
+
+    def sums_core_copy():
+        return wires.copy(first_sums, sums_held.at[...], sums_core, me.core)
+
+    sums_core_copy().start()
+    pulled = from_attn * vec_ref[0:1, :] + from_mlp * vec_ref[2:3, :]
+    pulled = (
+        pulled
+        - jnp.mean(pulled, axis=-1, keepdims=True)
+        - unit * jnp.mean(pulled * unit, axis=-1, keepdims=True)
+    )
+    input_grad_ref[...] = (cotangent + rate * pulled).astype(BF16)
+
+    sums_core_copy().wait()
+    sums_core[...] = sums_held[...] + sums_core[...]
+
+    def sums_cross_copy(which):
+        return wires.copy(
+            first_sums + 1 + which, sums_core, sums_cross.at[which], me.cross[which]
+        )
+
+    for which in range(3):
+        sums_cross_copy(which).start()
+    for which in range(3):
+        sums_cross_copy(which).wait()
+    sums_held[...] = sums_core[...] + sums_cross[0] + sums_cross[1] + sums_cross[2]
+
+    def sums_line_copy(step, block, origin):
+        return wires.copy(
+            first_sums + 4 + step - 1,
+            sums_held.at[:, rows_of(block, 256)],
+            sums_line.at[origin],
+            me.line((z + step) % LINE),
+        )
+
+    for step in range(1, LINE):
+        sums_line_copy(step, (z + step) % LINE, z).start()
+    sums_line[z] = sums_held[:, rows_of(z, 256)]
+
+    reduce_down.finish()
+    down_grad_ref[...] = down_held[z].astype(F32)
+    reduce_up.finish()
+    first_uf = wires.take(3)
+
+    def up_out_copy(which, origin):
+        peer = peers[which]
+        return wires.copy(
+            first_uf + which,
+            up_held.at[z, rows_of(peer, 64), :],
+            up_final.at[origin],
+            me.at(z, peer, t),
+        )
+
+    for which in range(3):
+        up_out_copy(which, k).start()
+    up_final[k] = up_held[z, rows_of(k, 64), :]
+
+    for which in range(3):
+        qkv_out_copy(which, peers[which]).wait_recv()
+    for origin in range(4):
+        qkv_grad_ref[:, :, origin * PAIR : (origin + 1) * PAIR] = qkv_final[origin].astype(F32)
+    for other in range(4):
+
+        @pl.when((k != z) | (z != other))
+        def _():
+            back_arrival(other, 0).wait_recv()
+            back_arrival(other, 1).wait_recv()
+
+    dense_grad_ref[...] = (
+        dense_final[0].astype(F32)
+        + dense_final[1].astype(F32)
+        + dense_final[2].astype(F32)
+        + dense_final[3].astype(F32)
+    )
+    for which in range(3):
+        up_out_copy(which, peers[which]).wait_recv()
+    for origin in range(4):
+        for other in range(LINE):
+            first = (other * 4 + origin) * 128
+            up_grad_ref[:, first : first + 128] = up_final[
+                origin, :, other * 128 : (other + 1) * 128
+            ].astype(F32)
+
+    for step in range(1, LINE):
+        sums_line_copy(step, z, (z + LINE - step) % LINE).wait_recv()
+        up_bias_copy(step, z, (z + LINE - step) % LINE).wait_recv()
+    sums = sums_line[0] + sums_line[1] + sums_line[2] + sums_line[3]
+    sums = jnp.where(k >= 2, sums[:, 128:], sums[:, :128])
+    small_out_ref[0:8, :] = pltpu.roll(sums, (128 - (me.q % 4) * 32) % 128, 1)
+    bias_sum = qkv_bias_final[0] + qkv_bias_final[1] + qkv_bias_final[2] + qkv_bias_final[3]
+    small_out_ref[8:16, :] = pltpu.roll(bias_sum, (128 - k * 32) % 128, 1)
+    small_out_ref[16:24, :] = (
+        up_bias_final[0] + up_bias_final[1] + up_bias_final[2] + up_bias_final[3]
+    )
+
+    for step in range(1, LINE):
+        small_copy(step, z).wait_send()
+        up_bias_copy(step, (z + step) % LINE, z).wait_send()
+        sums_line_copy(step, (z + step) % LINE, z).wait_send()
+    for which in range(3):
+        qkv_copy(which, k).wait_send()
+        qkv_out_copy(which, k).wait_send()
+        up_out_copy(which, k).wait_send()
+        for other in range(LINE):
+            up_copy(which, other, k).wait_send()
+    for other in range(4):
+
+        @pl.when((k != z) | (z != other))
+        def _():
+            dense_send(other).wait_send()
+
+        @pl.when((k != z) | (k != other))
+        def _():
+            back_send(other, 0).wait_send()
+            back_send(other, 1).wait_send()
+
+    for item in (
+        gather_x,
+        gather_g,
+        gather_small,
+        line_qkv,
+        line_mlp,
+        reduce_attn,
+        reduce_out,
+        reduce_mlp,
+        reduce_qkv,
+        reduce_down,
+        reduce_up,
+    ):
+        item.drain()
+
+
+def plane_layer(
+    hidden_in,
+    out_grad,
+    span_start,
+    span_length,
+    attn_gain,
+    attn_shift,
+    mlp_gain,
+    mlp_shift,
+    qkv_weight,
+    qkv_bias,
+    dense_weight,
+    dense_bias,
+    up_weight,
+    up_bias,
+    down_weight,
+    down_bias,
+):
+    smalls = jnp.concatenate(
+        [
+            attn_gain.astype(F32),
+            attn_shift.astype(F32),
+            mlp_gain.astype(F32),
+            mlp_shift.astype(F32),
+            dense_bias.astype(F32),
+            down_bias.astype(F32),
+            span_start[0].astype(F32),
+            span_length[0].astype(F32),
+            jnp.zeros((60,), F32),
+            qkv_bias.astype(F32).reshape(96),
+            jnp.zeros((32,), F32),
+            up_bias.astype(F32),
+            jnp.zeros((512,), F32),
+        ]
+    ).reshape(8, 128)
+    vmem = pl.BlockSpec(memory_space=pltpu.VMEM)
+    anywhere = pl.BlockSpec(memory_space=pl.ANY)
+    tokens = 4 * SEQ
+    outs = pl.pallas_call(
+        layer_kernel,
+        out_shape=(
+            jax.ShapeDtypeStruct((128, WIDTH), BF16),
+            jax.ShapeDtypeStruct((128, WIDTH), BF16),
+            jax.ShapeDtypeStruct((3, 64, 512), F32),
+            jax.ShapeDtypeStruct((32, WIDTH), F32),
+            jax.ShapeDtypeStruct((64, 2048), F32),
+            jax.ShapeDtypeStruct((128, WIDTH), F32),
+            jax.ShapeDtypeStruct((24, 128), F32),
+        ),
+        in_specs=[anywhere] * 7 + [vmem],
+        out_specs=(vmem,) * 7,
+        scratch_shapes=[
+            pltpu.VMEM((tokens, WIDTH), BF16),
+            pltpu.VMEM((tokens, WIDTH), BF16),
+            pltpu.VMEM((LINE, 8, 128), F32),
+            pltpu.VMEM((8, LINE, 8, 128), F32),
+            pltpu.VMEM((3, WIDTH, PAIR), BF16),
+            pltpu.VMEM((PAIR, WIDTH), BF16),
+            pltpu.VMEM((WIDTH, HID), BF16),
+            pltpu.VMEM((HID, WIDTH), BF16),
+            pltpu.VMEM((8, WIDTH), F32),
+            pltpu.VMEM((8, PAIR), F32),
+            pltpu.VMEM((tokens, WIDTH), BF16),
+            pltpu.VMEM((tokens, WIDTH), BF16),
+            pltpu.VMEM((tokens, PAIR), BF16),
+            pltpu.VMEM((tokens, 3 * PAIR), BF16),
+            pltpu.VMEM((tokens, HID), BF16),
+            pltpu.VMEM((tokens, HID), BF16),
+            pltpu.VMEM((tokens, WIDTH), BF16),
+            pltpu.VMEM((tokens, WIDTH), BF16),
+            pltpu.VMEM((tokens, WIDTH), BF16),
+            pltpu.VMEM((3, 2, SEQ, WIDTH), BF16),
+            pltpu.VMEM((3, 3, 128, WIDTH), BF16),
+            pltpu.VMEM((LINE, 256, HID), BF16),
+            pltpu.VMEM((2, LINE, 256, HID), BF16),
+            pltpu.VMEM((LINE, 128, WIDTH), BF16),
+            pltpu.VMEM((2, LINE, 128, WIDTH), BF16),
+            pltpu.VMEM((LINE, 3, 256, PAIR), BF16),
+            pltpu.VMEM((2, LINE, 3, 256, PAIR), BF16),
+            pltpu.VMEM((4, 64, HID), BF16),
+            pltpu.VMEM((4, 3, 64, PAIR), BF16),
+            pltpu.VMEM((PAIR, WIDTH), BF16),
+            pltpu.VMEM((LINE, 32, WIDTH), BF16),
+            pltpu.VMEM((8, PAIR), F32),
+            pltpu.VMEM((LINE, 8, PAIR), F32),
+            pltpu.VMEM((8, HID), F32),
+            pltpu.VMEM((LINE, 8, 128), F32),
+            pltpu.VMEM((8, WIDTH), F32),
+            pltpu.VMEM((8, WIDTH), F32),
+            pltpu.VMEM((3, 8, WIDTH), F32),
+            pltpu.VMEM((LINE, 8, 256), F32),
+            pltpu.SemaphoreType.DMA((160,)),
+            pltpu.SemaphoreType.DMA((160,)),
+            pltpu.SemaphoreType.DMA((16,)),
+        ],
+        compiler_params=pltpu.CompilerParams(
+            collective_id=0, has_side_effects=True, vmem_limit_bytes=60 * 2**20
+        ),
+    )(
+        hidden_in,
+        out_grad,
+        smalls,
+        jnp.transpose(qkv_weight, (1, 0, 2)),
+        dense_weight,
+        up_weight,
+        down_weight,
+        jnp.asarray(turn_tables()),
+    )
+    layer_out, input_grad, qkv_grad, dense_grad, up_grad, down_grad, small_out = outs
+    bias_total = small_out[4, :32]
+    return (
+        layer_out,
+        input_grad,
+        small_out[0, :32],
+        small_out[1, :32],
+        small_out[2, :32],
+        small_out[3, :32],
+        jnp.transpose(qkv_grad, (1, 0, 2)),
+        small_out[8:11, :32],
+        dense_grad,
+        bias_total,
+        up_grad,
+        small_out[16],
+        down_grad,
+        bias_total,
+    )
+
+
 def solution(mesh):
     in_specs = (
         P(("dp", "tensor"), None),
@@ -296,4 +1369,5 @@
         P(("tensor", "dp"), None),
         P(("dp", "tensor")),
     )
-    return jax.shard_map(shards, mesh=mesh, in_specs=in_specs, out_specs=out_specs, check_vma=False)
+    fast = mesh.shape["dp"] == 16 and mesh.shape["tensor"] == 2
+    return jax.shard_map(plane_layer if fast else shards, mesh=mesh, in_specs=in_specs, out_specs=out_specs, check_vma=False)

time: 705 us -> 209 us (0.30)
  waiting for transfers between devices: 425 us -> 0 us
  Pallas kernels: 0 us -> 194 us
  blocking collectives: 176 us -> 0 us
  matrix products: 48.5 us -> 0 us
  other arithmetic: 14.6 us -> 0.01 us
  between operations: 15 us -> 0.74 us
  local copies, waits for them, and re-layouts: 24.5 us -> 13.6 us
    reduce_scatter x8 -> x0, waiting for transfers between devices: 359 us -> none  [the longest x1 109 us: shards(): lax.psum_scatter(up_grad, 'dp', scatter_dimension=0, tiled=True)]
    pallas_call x0 -> x1, Pallas kernels: none -> 194 us  [plane_layer(): pl.pallas_call(layer_kernel, out_shape=(jax.ShapeDtypeStruct((128, WIDTH)...]
    unnamed x3 -> x0, blocking collectives: 112 us -> none
    all_gather x5 -> x0, blocking collectives: 64.2 us -> none  [the longest x1 21.3 us: shards(): lax.all_gather(qkv_bias, 'dp', axis=1, tiled=True)]
    dot_general x18 -> x0, matrix products: 48.5 us -> none  [the longest x1 9.03 us: shards(): jnp.einsum('ld,fd->lf', cot_full, full_down, preferred_element_type=jnp.f...]
    all_gather x4 -> x0, waiting for transfers between devices: 44.1 us -> none  [the longest x1 44.1 us: shards(): lax.all_gather(down_weight, 'dp', axis=0, tiled=True)]
    unnamed x14 -> x0, waiting for transfers between devices: 21 us -> none
    reduce_sum x8 -> x0, other arithmetic: 8.9 us -> none  [the longest x2 2.92 us: layer_norm(): return centred * lax.rsqrt(spread + NORM_EPS) * gain_vec + shift_vec]
  transfers between devices with their start and end apart: 13 -> 0, of which waited for: 9 -> 0; matrix products, arithmetic and copies ran while one was open for 12% -> 0% of each run, Pallas kernels for 0% -> 0%
where the time goes in v1:
time: 209 us
  Pallas kernels  194 us (93%)
  local copies, waits for them, and re-layouts  13.6 us (7%)
    pallas_call x1, Pallas kernels, plane_layer(): pl.pallas_call(layer_kernel, out_shape=(jax.ShapeDtypeStruct((128, WIDTH)...  194 us
    unnamed x39, local copies, waits for them, and re-layouts  9.06 us

profile of v1, /device:TPU:0, one launch (start us, length us, event | category | flops | bytes accessed | tf_op | source)
XLA Modules:
  0.0 208.9 jit_solution(10914805436112996186)
XLA Ops:
  0.7 0.7 copy-done.15
  1.3 0.1 reshape.43
  1.4 0.6 copy-done.13
  2.0 0.0 copy-done.14
  2.0 0.0 copy-start.11
  2.0 0.0 copy-start.5
  2.0 0.0 copy-start.6
  2.1 0.0 copy-start.7
  2.1 0.0 copy-start.8
  2.1 0.0 copy-start.9
  2.1 0.6 copy-done.10
  2.7 0.0 copy-done.11
  2.7 0.0 copy-done.5
  2.7 0.0 copy-done.6
  2.7 0.0 copy-done.7
  2.7 0.0 copy-done.8
  2.7 0.0 copy-done.9
  2.8 0.7 concatenate.3
  3.4 194.5 %shard_map.272 = (bf16[128,1024]{1,0:T(8,128)(2,1)}, bf16[128,1024]{1,0:T(8,128)(2,1)}, f32[3,64,512]{2,1,0:T(8,128)}, f32[32,1024]{1,0:T(8,128)}, f32[64,2048]{...) custom-call(bf16[128,1024]{1,0:T(8,128)(2,1)} %x_hbm.1, bf16[128,1024]{1,0:T(8,128)(2,1)} %g_hbm.1, ...), custom_call_target="tpu_custom_call" | custom-call | tf_op jit(solution)/shard_map/pallas_call | solution.py:1247
  197.9 1.2 slice_bitcast_fusion
  199.1 1.3 slice.25
  200.4 1.4 slice_bitcast_fusion.1
  201.7 0.5 copy-done.12
  202.3 0.5 copy.38
  202.8 1.7 copy.39
  204.5 0.7 copy.40
  205.2 0.7 copy.41
  205.9 0.2 copy-done.4
  206.2 0.7 copy.42
  206.9 0.8 copy.43
  207.7 0.4 copy-done
  208.1 0.8 copy.44
  (17 shorter events, 0.0 us)
Async XLA Ops:
  0.6 0.7 copy-start.15
  1.3 0.7 copy-start.13
  1.3 0.7 copy-start.14
  2.0 0.7 copy-start.10
  2.0 0.7 copy-start.11
  2.0 0.7 copy-start.5
  2.0 0.7 copy-start.6
  2.1 0.7 copy-start.7
  2.1 0.7 copy-start.8
  2.1 0.7 copy-start.9
  201.7 0.5 copy-start.12
  201.7 2.7 %copy-start.3 = (bf16[128,1024]{1,0:T(8,128)(2,1)S(1)}, bf16[128,1024]{1,0:T(8,128)(2,1)}, u32[]{:S(2)}) copy-start(bf16[128,1024]{1,0:T(8,128)(2,1)} %get-tuple-element.78) | copy-start | bytes 786436
  202.8 2.4 %copy-start.2 = (f32[3,64,512]{2,1,0:T(8,128)S(1)}, f32[3,64,512]{2,1,0:T(8,128)}, u32[]{:S(2)}) copy-start(f32[3,64,512]{2,1,0:T(8,128)} %get-tuple-element.24) | copy-start | bytes 1179652
  205.2 1.0 copy-start.4
  205.2 1.7 copy-start.1
  206.9 1.2 copy-start

commit v2 on v0

--- a/solution.py
+++ b/solution.py
@@ -1,6 +1,9 @@
 import jax
 import jax.numpy as jnp
+import numpy as np
 from jax import lax
+from jax.experimental import pallas as pl
+from jax.experimental.pallas import tpu as pltpu
 from jax.sharding import PartitionSpec as P
 
 HD = 64
@@ -261,6 +264,1273 @@
     )
 
 
+F32 = jnp.float32
+BF16 = jnp.bfloat16
+MESH_ID = pl.DeviceIdType.MESH
+LINE = 4
+SEQ = 256
+WIDTH = 1024
+HID = 512
+PAIR = 128
+
+
+def nn(a, b):
+    return jnp.dot(a, b, preferred_element_type=F32)
+
+
+def nt(a, b):
+    return lax.dot_general(a, b, (((1,), (1,)), ((), ())), preferred_element_type=F32)
+
+
+def tn(a, b):
+    return lax.dot_general(a, b, (((0,), (0,)), ((), ())), preferred_element_type=F32)
+
+
+def turn_tables():
+    position = np.arange(SEQ, dtype=np.float64)[:, None]
+    lane = np.arange(PAIR) % HD
+    rates = 10000.0 ** (-(lane % (ROT // 2)) * (2.0 / ROT))
+    angles = position * rates[None, :]
+    cosine = np.where(lane < ROT, np.cos(angles), 1.0)
+    toward = np.where(lane < ROT // 2, -np.sin(angles), 0.0)
+    away = np.where((lane >= ROT // 2) & (lane < ROT), np.sin(angles), 0.0)
+    return np.stack([cosine, toward, away]).astype(np.float32)
+
+
+SEATS = (0, 3, 1, 2)
+
+
+def seat_of(z):
+    return (2 * z - z // 2) % LINE
+
+
+def rows_of(index, count):
+    return pl.ds(pl.multiple_of(index * count, count), count)
+
+
+class Place:
+    def __init__(self):
+        index = lax.axis_index("dp")
+        self.t = lax.axis_index("tensor")
+        self.z = index // 4
+        self.k = index % 4
+        self.y = self.k // 2
+        self.c = self.k % 2
+        self.kc = self.y * 2 + 1 - self.c
+        self.ky = (1 - self.y) * 2 + self.c
+        self.kyc = (1 - self.y) * 2 + 1 - self.c
+        self.q = self.k * 2 + self.t
+        self.core = self.at(self.z, self.kc, self.t)
+        self.cross = (
+            self.at(self.z, self.k, 1 - self.t),
+            self.at(self.z, self.ky, self.t),
+            self.at(self.z, self.ky, 1 - self.t),
+        )
+
+    def at(self, z, k, t):
+        return (z * 4 + k, t)
+
+    def line(self, z):
+        return self.at(z, self.k, self.t)
+
+
+class Wires:
+    def __init__(self, sends, arrivals):
+        self.sends, self.arrivals = sends, arrivals
+        self.sent, self.landed = 0, 0
+
+    def take(self, sends, arrivals):
+        first = (self.sent, self.landed)
+        self.sent += sends
+        self.landed += arrivals
+        return first
+
+    def copy(self, send, arrival, src, dst, device):
+        return pltpu.make_async_remote_copy(
+            src_ref=src,
+            dst_ref=dst,
+            send_sem=self.sends.at[send],
+            recv_sem=self.arrivals.at[arrival],
+            device_id=device,
+            device_id_type=MESH_ID,
+        )
+
+    def all_sent(self, send, view, device):
+        self.copy(send, 0, view, view, device).wait_send()
+
+    def all_landed(self, arrival, view, device):
+        self.copy(0, arrival, view, view, device).wait_recv()
+
+
+class PlaneGather:
+    def __init__(self, me, wires, src, slot, split, blocks):
+        self.me, self.wires, self.src, self.slot = me, wires, src, slot
+        self.blocks = blocks
+        self.pieces = (pl.ds(0, split), pl.ds(split, src.shape[0] - split))
+        self.send, self.arrivals = wires.take(1, 4)
+        self.near_blocks = (
+            me.k * 2 + 1 - me.t,
+            me.ky * 2 + me.t,
+            me.ky * 2 + 1 - me.t,
+        )
+
+    def start(self, which):
+        device = (self.me.cross[0], self.me.cross[1], self.me.core)[which]
+        arrival = self.arrivals + (0, 1, 3)[which]
+        self.wires.copy(self.send, arrival, self.src, self.slot(self.me.q), device).start()
+
+    def pass_on(self, which):
+        part = self.slot(self.near_blocks[which])
+        self.wires.copy(self.send, self.arrivals + 3, part, part, self.me.core).start()
+
+    def forward(self, which):
+        block = self.slot(self.near_blocks[which])
+        self.wires.all_landed(self.arrivals + which, block, self.me.core)
+        part = block.at[self.pieces[which]]
+        device = self.me.cross[1 - which]
+        self.wires.copy(self.send, self.arrivals + 2, part, part, device).start()
+        self.pass_on(which)
+
+    def corner(self):
+        block = self.slot(self.near_blocks[2])
+        self.wires.all_landed(self.arrivals + 2, block, self.me.core)
+        self.pass_on(2)
+
+    def finish(self):
+        self.wires.all_landed(self.arrivals + 3, self.blocks(4), self.me.core)
+
+    def drain(self):
+        self.wires.all_sent(self.send, self.blocks(7), self.me.core)
+
+
+class LineGather:
+    def __init__(self, me, wires, view):
+        self.me, self.wires, self.view = me, wires, view
+        self.sends, self.arrivals = wires.take(2, 6)
+
+    def copy(self, way, hop, block):
+        z = self.me.z
+        view = self.view(block, 1)
+        device = self.me.line(z + 1 if way == 0 else z - 1)
+        return self.wires.copy(self.sends + way, self.arrivals + way * 3 + hop, view, view, device)
+
+    def send(self, way, hop):
+        z = self.me.z
+        has = (z >= hop) & (z < LINE - 1) if way == 0 else (z + hop < LINE) & (z > 0)
+
+        @pl.when(has)
+        def _():
+            self.copy(way, hop, z - hop if way == 0 else z + hop).start()
+
+    def arrive(self, way, hop):
+        z = self.me.z
+
+        @pl.when(z > hop if way == 0 else z + 1 + hop < LINE)
+        def _():
+            self.copy(way, hop, z - 1 - hop if way == 0 else z + 1 + hop).wait_recv()
+
+    def start(self, way):
+        @pl.when(self.me.z != (0 if way == 0 else LINE - 1))
+        def _():
+            self.send(way, 0)
+
+    def outer(self):
+        for way in range(2):
+
+            @pl.when(self.me.z == (0 if way == 0 else LINE - 1))
+            def _(way=way):
+                self.send(way, 0)
+
+    def relay(self, way, hop):
+        self.arrive(way, hop - 1)
+        self.send(way, hop)
+
+    def finish(self, way):
+        self.arrive(way, LINE - 2)
+
+    def drain(self):
+        z = self.me.z
+        for way in range(2):
+            for count in range(1, LINE):
+
+                @pl.when(z == (count - 1 if way == 0 else LINE - count))
+                def _():
+                    self.wires.all_sent(self.sends + way, self.view(0, count), self.me.core)
+
+
+class LineReduce:
+    def __init__(self, me, wires, held, landed):
+        self.me, self.wires, self.held, self.landed = me, wires, held, landed
+        self.sends, self.arrivals = wires.take(2, 6)
+
+    def copy(self, way, block):
+        z = self.me.z
+        device = self.me.line(z - 1 if way == 0 else z + 1)
+        return self.wires.copy(
+            self.sends + way,
+            self.arrivals + way * (LINE - 2) + block,
+            self.held.at[block],
+            self.landed.at[way, block],
+            device,
+        )
+
+    def join(self, way, block):
+        self.copy(way, block).wait_recv()
+        total = self.held[block].astype(F32) + self.landed[way, block].astype(F32)
+        self.held[block] = total.astype(BF16)
+
+    def each(self, way, slot, act):
+        z = self.me.z
+        steps = slot - (LINE - 1 - z if way == 0 else z)
+        left = z if way == 0 else LINE - 1 - z
+        block = steps if way == 0 else LINE - 1 - steps
+
+        @pl.when((steps >= 0) & (steps < left))
+        def _():
+            act(block)
+
+    def slot(self, way, slot):
+        def act(block):
+            if slot > 0:
+                started = self.me.z < LINE - 1 if way == 0 else self.me.z > 0
+
+                @pl.when(started)
+                def _():
+                    self.join(way, block)
+
+            self.copy(way, block).start()
+
+        self.each(way, slot, act)
+
+    def finish(self, way):
+        z = self.me.z
+
+        @pl.when(z < LINE - 1 if way == 0 else z > 0)
+        def _():
+            self.join(way, z)
+
+    def drain(self):
+        z = self.me.z
+        for way in range(2):
+            for count in range(1, LINE):
+
+                @pl.when(z == (count if way == 0 else LINE - 1 - count))
+                def _():
+                    view = self.held.at[pl.ds(0, count)]
+                    self.wires.all_sent(self.sends + way, view, self.me.core)
+
+
+class PlaneReduce:
+    def __init__(self, me, wires, part, paired, crossed):
+        self.me, self.wires = me, wires
+        self.part, self.paired, self.crossed = part, paired, crossed
+        self.send, self.arrivals = wires.take(1, 4)
+        self.blocks = (me.ky * 2 + 1 - me.t, me.k * 2 + 1 - me.t, me.ky * 2 + me.t)
+
+    def pair(self, y):
+        rows = rows_of(y * 2 + 1 - self.me.c, SEQ)
+        return self.wires.copy(
+            self.send, self.arrivals, self.part.at[rows], self.paired.at[y], self.me.core
+        )
+
+    def rows(self, which, half):
+        first = pl.multiple_of(self.blocks[which] * 128 + half * 64, 64)
+        return pl.ds(first, 64)
+
+    def cross(self, which, half):
+        way = (half, 0, 1)[which]
+        return self.wires.copy(
+            self.send,
+            self.arrivals + (1 + half if which == 0 else 3),
+            self.part.at[self.rows(which, half)],
+            self.crossed.at[which, pl.ds(half * 64, 64)],
+            self.me.cross[way],
+        )
+
+    def middle(self):
+        self.wires.all_landed(self.arrivals, self.part.at[pl.ds(0, 2 * SEQ)], self.me.core)
+        for y in range(2):
+            rows = rows_of(y * 2 + self.me.c, SEQ)
+            total = self.part[rows].astype(F32) + self.paired[y].astype(F32)
+            self.part[rows] = total.astype(BF16)
+        for which, half in ((0, 0), (0, 1), (1, 0), (2, 1)):
+            self.cross(which, half).start()
+
+    def turn(self, half):
+        self.cross(0, half).wait_recv()
+        rows = self.rows(2 - half, half)
+        total = self.part[rows].astype(F32) + self.crossed[0, pl.ds(half * 64, 64)].astype(F32)
+        self.part[rows] = total.astype(BF16)
+        self.cross(2 - half, half).start()
+
+    def finish(self):
+        self.wires.all_landed(self.arrivals + 3, self.part.at[pl.ds(0, SEQ)], self.me.core)
+        total = self.part[rows_of(self.me.q, 128)].astype(F32)
+        return total + self.crossed[1].astype(F32) + self.crossed[2].astype(F32)
+
+    def drain(self):
+        self.wires.all_sent(self.send, self.part.at[pl.ds(0, 896)], self.me.core)
+
+
+def layer_kernel(
+    x_hbm,
+    g_hbm,
+    qkv_hbm,
+    dense_hbm,
+    up_hbm,
+    down_hbm,
+    turn_hbm,
+    attn_gain_ref,
+    attn_shift_ref,
+    mlp_gain_ref,
+    mlp_shift_ref,
+    dense_bias_ref,
+    down_bias_ref,
+    starts_ref,
+    lengths_ref,
+    qkv_bias_ref,
+    up_bias_ref,
+    layer_out_ref,
+    input_grad_ref,
+    qkv_grad_ref,
+    dense_grad_ref,
+    up_grad_ref,
+    down_grad_ref,
+    small_out_ref,
+    turn_ref,
+    x_all,
+    g_all,
+    small_line,
+    small_all,
+    qkv_w,
+    dense_w,
+    up_w,
+    down_w,
+    vec_ref,
+    bias_ref,
+    normed_a,
+    normed_m,
+    context_ref,
+    turned_grad,
+    active_ref,
+    hidden_grad,
+    slope_ref,
+    part_out,
+    part_attn,
+    part_mlp,
+    paired_ref,
+    crossed_ref,
+    up_held,
+    up_landed,
+    down_held,
+    down_landed,
+    qkv_held,
+    qkv_landed,
+    up_final,
+    qkv_final,
+    dense_line,
+    dense_held,
+    dense_mine,
+    dense_landed,
+    qkv_bias_held,
+    qkv_bias_line,
+    qkv_bias_final,
+    up_bias_held,
+    up_bias_final,
+    sums_held,
+    sums_chip,
+    sums_total,
+    sums_core,
+    sums_cross,
+    sums_line,
+    sends,
+    arrivals,
+    local_sems,
+):
+    me = Place()
+    wires = Wires(sends, arrivals)
+    z, k, t = me.z, me.k, me.t
+
+    barrier = pltpu.get_barrier_semaphore()
+
+    def greet(device):
+        pl.semaphore_signal(barrier, inc=1, device_id=device, device_id_type=MESH_ID)
+
+    greet(me.core)
+    greet(me.at(z, me.kyc, t))
+    for device in me.cross:
+        greet(device)
+    for step in range(1, LINE):
+        greet(me.line((z + step) % LINE))
+    local_copies = []
+
+    def local(src, dst):
+        copy = pltpu.make_async_copy(src, dst, local_sems.at[len(local_copies)])
+        local_copies.append(copy)
+        copy.start()
+
+    seat = pl.ds(pl.multiple_of(z * 256 + k * 64, 64), 64)
+    peers = (me.kc, me.ky, me.kyc)
+    devices = tuple(me.at(z, peer, t) for peer in peers)
+
+    def three(arrival, view):
+        wires.all_landed(arrival, view, me.core)
+
+    local(dense_hbm, dense_line.at[z])
+    for place, other in enumerate(SEATS):
+        local(
+            up_hbm.at[:, rows_of(other * 4 + k, 128)],
+            up_w.at[seat, pl.ds(place * 128, 128)],
+        )
+    local(down_hbm, down_w.at[rows_of(seat_of(z), 128)])
+    for which in range(3):
+        local(
+            qkv_hbm.at[which, :, rows_of(k, PAIR)],
+            qkv_w.at[seat, pl.ds(which * PAIR, PAIR)],
+        )
+    local(x_hbm, x_all.at[rows_of(me.q, 128)])
+    local(g_hbm, g_all.at[rows_of(me.q, 128)])
+    local(turn_hbm, turn_ref)
+    qkv_bias_held[...] = jnp.zeros_like(qkv_bias_held)
+    up_bias_held[...] = jnp.zeros_like(up_bias_held)
+
+    def side_by_side(*fields):
+        return jnp.concatenate(
+            [field.astype(F32).reshape(1, field.shape[-1]) for field in fields], axis=1
+        )
+
+    triple = qkv_bias_ref[...]
+    blank = jnp.zeros((1, 60), F32)
+    small_line[z] = jnp.concatenate(
+        [
+            side_by_side(
+                attn_gain_ref[...], attn_shift_ref[...], mlp_gain_ref[...], mlp_shift_ref[...]
+            ),
+            side_by_side(
+                dense_bias_ref[...], down_bias_ref[...], starts_ref[...], lengths_ref[...], blank
+            ),
+            side_by_side(triple[0:1], triple[1:2], triple[2:3], blank[:, :32]),
+            side_by_side(up_bias_ref[...]),
+            jnp.zeros((4, 128), F32),
+        ],
+        axis=0,
+    )
+    pl.semaphore_wait(barrier, 8)
+
+    up_send, up_arrival = wires.take(1, 2)
+    for place, other in enumerate(SEATS):
+        for which in range(3):
+            wires.copy(
+                up_send,
+                up_arrival + place // 2,
+                up_hbm.at[:, rows_of(other * 4 + peers[which], 128)],
+                up_w.at[seat, pl.ds(place * 128, 128)],
+                devices[which],
+            ).start()
+
+    qkv_sends, qkv_arrival = wires.take(1, 1)
+
+    def rows_slot(ref):
+        return (lambda block: ref.at[rows_of(block, 128)]), (
+            lambda count: ref.at[pl.ds(0, count * 128)]
+        )
+
+    slot, blocks = rows_slot(x_all)
+    gather_x = PlaneGather(me, wires, x_hbm, slot, 48, blocks)
+    for which in range(3):
+        gather_x.start(which)
+    slot, blocks = rows_slot(g_all)
+    gather_g = PlaneGather(me, wires, g_hbm, slot, 48, blocks)
+    gather_small = PlaneGather(
+        me,
+        wires,
+        small_line,
+        lambda block: small_all.at[block],
+        2,
+        lambda count: small_all.at[pl.ds(0, count)],
+    )
+    small_send, small_arrival = wires.take(1, 1)
+    for step in range(1, LINE):
+        wires.copy(
+            small_send,
+            small_arrival,
+            small_line.at[z],
+            small_line.at[z],
+            me.line((z + step) % LINE),
+        ).start()
+
+    def line_gather(ref, count):
+        return LineGather(
+            me, wires, lambda s, n: ref.at[pl.ds(pl.multiple_of(s * count, count), n * count)]
+        )
+
+    line_dense = LineGather(me, wires, lambda s, n: dense_line.at[pl.ds(s, n)])
+    line_qkv = line_gather(qkv_w, 256)
+    line_upa, line_upb = (
+        LineGather(
+            me,
+            wires,
+            lambda s, n, first=first: up_w.at[
+                pl.ds(pl.multiple_of(s * 256, 256), n * 256), pl.ds(first, 256)
+            ],
+        )
+        for first in (0, 256)
+    )
+    line_down = LineGather(
+        me,
+        wires,
+        lambda s, n: down_w.at[pl.ds(pl.multiple_of(seat_of(s) * 128, 128), n * 128)],
+    )
+    reduce_down = LineReduce(
+        me, wires, down_held, down_landed
+    )
+    reduce_up = LineReduce(
+        me, wires, up_held, up_landed
+    )
+    reduce_qkv = LineReduce(
+        me, wires, qkv_held, qkv_landed
+    )
+    reduce_dense = LineReduce(
+        me, wires, dense_mine, dense_landed
+    )
+    reduce_attn = PlaneReduce(me, wires, part_attn, paired_ref.at[0], crossed_ref.at[0])
+    reduce_out = PlaneReduce(me, wires, part_out, paired_ref.at[1], crossed_ref.at[1])
+    reduce_mlp = PlaneReduce(me, wires, part_mlp, paired_ref.at[2], crossed_ref.at[2])
+
+    local_copies[0].wait()
+    line_dense.outer()
+    line_dense.start(0)
+    line_dense.start(1)
+
+    own_small = pltpu.make_async_copy(
+        small_line, small_all.at[me.q], local_sems.at[len(local_copies)]
+    )
+    own_dense = pltpu.make_async_copy(
+        dense_line.at[k], dense_w.at[rows_of(k, 32)], local_sems.at[len(local_copies) + 1]
+    )
+    dense_sends, dense_arrival = wires.take(1, 1)
+    back_sends, back_arrival = wires.take(2, 2)
+    bias_sends, bias_arrival = wires.take(2, 2)
+    out_sends, out_arrival = wires.take(2, 2)
+    sums_sends, sums_arrival = wires.take(3, 3)
+
+    def along(send, arrival, source, target):
+        for step in range(1, LINE):
+            there = (z + step) % LINE
+            wires.copy(send, arrival, source(there), target, me.line(there)).start()
+
+    def around(send, arrival, source, target):
+        for which in range(3):
+            wires.copy(send, arrival, source(peers[which]), target, devices[which]).start()
+
+    def norm_rows(rows):
+        values = x_all[rows].astype(F32)
+        centred = values - jnp.mean(values, axis=-1, keepdims=True)
+        rate = lax.rsqrt(jnp.mean(centred * centred, axis=-1, keepdims=True) + NORM_EPS)
+        return centred * rate, rate
+
+    def norm_block(block, carry):
+        rows = rows_of(block, 128)
+        unit, _ = norm_rows(rows)
+        normed_a[rows] = (unit * vec_ref[0:1, :] + vec_ref[1:2, :]).astype(BF16)
+        normed_m[rows] = (unit * vec_ref[2:3, :] + vec_ref[3:4, :]).astype(BF16)
+        return carry
+
+    def activate(half):
+        columns = slice(half * 256, (half + 1) * 256)
+
+        def tile_of(tile, carry):
+            rows = rows_of(tile, 256)
+            up_bias = jnp.concatenate(
+                [small_all[me.q, s, 3:4, :] for s in SEATS[half * 2 : half * 2 + 2]], axis=1
+            )
+            hidden = nn(normed_m[rows], up_w[:, columns]) + up_bias
+            share = (1.0 + lax.erf(hidden * 0.5**0.5)) * 0.5
+            bell = jnp.exp(hidden * hidden * -0.5) * (2.0 * np.pi) ** -0.5
+            slope_ref[rows, columns] = share + hidden * bell
+            active_ref[rows, columns] = (hidden * share).astype(BF16)
+            return carry
+
+        return tile_of
+
+    activate_a, activate_b = activate(0), activate(1)
+
+    def down_block(block, carry):
+        units = rows_of(seat_of(block), 128)
+        down_held[block] = tn(active_ref[:, units], g_all[...]).astype(BF16)
+        return carry
+
+    def feed_back(tile, carry):
+        rows = rows_of(tile, 256)
+        grad = (nt(g_all[rows], down_w[...]) * slope_ref[rows]).astype(BF16)
+        hidden_grad[rows] = grad
+        up_bias_held[0:1, :] += jnp.sum(grad.astype(F32), axis=0, keepdims=True)
+        return carry
+
+    def feed_in(tile, carry):
+        rows = rows_of(tile, 256)
+        part_mlp[rows] = nt(hidden_grad[rows], up_w[...]).astype(BF16)
+        return carry
+
+    def up_block(block, carry):
+        up_held[block] = tn(normed_m[:, rows_of(block, 256)], hidden_grad[...]).astype(BF16)
+        return carry
+
+    scale = HD**-0.5
+
+    def attend(seq, carry):
+        rows = rows_of(seq, SEQ)
+        cosine, toward, away = turn_ref[0], turn_ref[1], turn_ref[2]
+        projected = nn(normed_a[rows], qkv_w[...]) + bias_ref[0:1, :]
+
+        def project(which):
+            return projected[:, which * PAIR : (which + 1) * PAIR]
+
+        def turned(field):
+            return (
+                field * cosine
+                + pltpu.roll(field, ROT // 2, 1) * away
+                + pltpu.roll(field, PAIR - ROT // 2, 1) * toward
+            )
+
+        def turned_back(field):
+            return (
+                field * cosine
+                - pltpu.roll(field, ROT // 2, 1) * away
+                - pltpu.roll(field, PAIR - ROT // 2, 1) * toward
+            )
+
+        query = turned(project(0)).astype(BF16)
+        key = turned(project(1)).astype(BF16)
+        value = project(2).astype(BF16)
+        context_grad = nt(g_all[rows], dense_w[...]).astype(BF16)
+
+        spans = small_all[seq * 2, z, 1:2, :]
+        down_pos = lax.broadcasted_iota(jnp.int32, (SEQ, 1), 0).astype(F32)
+        over_pos = lax.broadcasted_iota(jnp.int32, (1, SEQ), 1).astype(F32)
+
+        def labels(place):
+            total = jnp.zeros(place.shape, F32)
+            for span in range(2):
+                begin = spans[:, 64 + span : 65 + span]
+                end = begin + spans[:, 66 + span : 67 + span]
+                total = total + jnp.where((place >= begin) & (place < end), span + 1.0, 0.0)
+            return total
+
+        down_label, over_label = labels(down_pos), labels(over_pos)
+        allowed = (over_pos <= down_pos) | ((down_label == over_label) & (down_label > 0.0))
+
+        lane = lax.broadcasted_iota(jnp.int32, (SEQ, PAIR), 1)
+        parts = []
+        for head in range(2):
+            mine = (lane >= HD) if head else (lane < HD)
+            zero = jnp.zeros_like(query)
+            scores = nt(jnp.where(mine, query, zero), key) * scale
+            scores = jnp.where(allowed, scores, NEG_FILL)
+            exponent = jnp.exp(scores - jnp.max(scores, axis=-1, keepdims=True))
+            probs = exponent * (1.0 / jnp.sum(exponent, axis=-1, keepdims=True))
+            low = probs.astype(BF16)
+            prob_grad = nt(jnp.where(mine, context_grad, zero), value)
+            inner = jnp.sum(prob_grad * probs, axis=-1, keepdims=True)
+            score_grad = (probs * (prob_grad - inner)).astype(BF16)
+            parts.append(
+                (
+                    nn(low, value),
+                    tn(low, context_grad),
+                    nn(score_grad, key) * scale,
+                    tn(score_grad, query) * scale,
+                )
+            )
+        context, value_grad, query_grad, key_grad = (
+            jnp.where(lane < HD, first, second) for first, second in zip(*parts)
+        )
+        context_ref[rows] = context.astype(BF16)
+        grads = (
+            turned_back(query_grad).astype(BF16),
+            turned_back(key_grad).astype(BF16),
+            value_grad.astype(BF16),
+        )
+        for which in range(3):
+            turned_grad[rows, which * PAIR : (which + 1) * PAIR] = grads[which]
+            qkv_bias_held[which : which + 1, :] += jnp.sum(
+                grads[which].astype(F32), axis=0, keepdims=True
+            )
+        part_attn[rows] = nt(turned_grad[rows], qkv_w[...]).astype(BF16)
+        return carry
+
+    def qkv_block(block, carry):
+        qkv_held[block] = tn(normed_a[:, rows_of(block, 256)], turned_grad[...]).astype(BF16)
+        return carry
+
+    def mix(tile, carry):
+        rows = rows_of(tile, 256)
+        mixed = nn(context_ref[rows], dense_w[...]) + nn(active_ref[rows], down_w[...])
+        part_out[rows] = mixed.astype(BF16)
+        return carry
+
+    def locals_done():
+        for copy in local_copies[1:]:
+            copy.wait()
+
+    def small_line_done():
+        three(small_arrival, small_line.at[pl.ds(0, 3)])
+        own_small.start()
+        for which in range(3):
+            gather_small.start(which)
+
+    def upa_start():
+        three(up_arrival, up_w.at[pl.ds(0, 96)])
+        line_upa.outer()
+        line_upa.start(0)
+        line_upa.start(1)
+
+    def upb_start():
+        three(up_arrival + 1, up_w.at[pl.ds(0, 96)])
+        line_upb.outer()
+        line_upb.start(0)
+        line_upb.start(1)
+
+    def down_outer():
+        line_down.outer()
+
+    def qkv_send():
+        for which in range(3):
+            for part in range(3):
+                wires.copy(
+                    qkv_sends,
+                    qkv_arrival,
+                    qkv_hbm.at[part, :, rows_of(peers[which], PAIR)],
+                    qkv_w.at[seat, pl.ds(part * PAIR, PAIR)],
+                    devices[which],
+                ).start()
+
+    def qkv_outer():
+        three(qkv_arrival, qkv_w.at[pl.ds(0, 192)])
+        line_qkv.outer()
+
+    def qkv_start():
+        line_qkv.start(0)
+        line_qkv.start(1)
+
+    def down_start():
+        line_down.start(0)
+        line_down.start(1)
+
+    def dense_send():
+        around(
+            dense_sends, dense_arrival, lambda to: dense_line.at[to], dense_w.at[rows_of(k, 32)]
+        )
+        own_dense.start()
+
+    def dense_done():
+        three(dense_arrival, dense_w.at[pl.ds(0, 96)])
+        own_dense.wait()
+
+    def vectors():
+        own_small.wait()
+        table = small_all[...].reshape(256, 128).astype(BF16)
+        line_id = lax.broadcasted_iota(jnp.int32, (256, WIDTH), 0)
+        column = lax.broadcasted_iota(jnp.int32, (256, WIDTH), 1)
+        owner = ((line_id >> 3) & 3) * 8 + (line_id >> 5)
+        lane_row = lax.broadcasted_iota(jnp.int32, (128, WIDTH), 0)
+        lane_col = lax.broadcasted_iota(jnp.int32, (128, WIDTH), 1) & 31
+        for kind, count, base in ((0, 4, 0), (1, 2, 4)):
+            chosen = (owner == (column >> 5)) & ((line_id & 7) == kind)
+            spread = tn(table, jnp.where(chosen, 1.0, 0.0).astype(BF16))
+            for which in range(count):
+                picked = jnp.where(lane_row == lane_col + which * 32, spread, 0.0)
+                vec_ref[base + which : base + which + 1, :] = jnp.sum(picked, axis=0, keepdims=True)
+        line_id = line_id[:, :PAIR]
+        column = column[:, :PAIR]
+        chosen = (
+            (((line_id >> 3) & 3) == k)
+            & ((line_id >> 5) == (column >> 5) * 2 + t)
+            & ((line_id & 7) == 2)
+        )
+        spread = tn(table, jnp.where(chosen, 1.0, 0.0).astype(BF16))
+        for which in range(3):
+            picked = jnp.where(lane_row[:, :PAIR] == lane_col[:, :PAIR] + which * 32, spread, 0.0)
+            total = jnp.sum(picked, axis=0, keepdims=True)
+            bias_ref[0:1, which * PAIR : (which + 1) * PAIR] = total
+
+    def up_bias_send():
+        along(
+            bias_sends,
+            bias_arrival,
+            lambda there: up_bias_held.at[:, rows_of(seat_of(there), 128)],
+            up_bias_final.at[z],
+        )
+        up_bias_final[z] = up_bias_held[:, rows_of(seat_of(z), 128)]
+
+    def dense_part():
+        dense_held[...] = tn(context_ref[...], g_all[...]).astype(BF16)
+        around(
+            back_sends, back_arrival, lambda to: dense_held.at[rows_of(to, 32)], dense_mine.at[k]
+        )
+        around(back_sends + 1, back_arrival + 1, lambda to: qkv_bias_held, qkv_bias_line.at[k])
+        dense_mine[k] = dense_held[rows_of(k, 32)]
+        qkv_bias_line[k] = qkv_bias_held[...]
+
+    def dense_back():
+        three(back_arrival, dense_mine.at[pl.ds(0, 3)])
+        three(back_arrival + 1, qkv_bias_line.at[pl.ds(0, 3)])
+        along(
+            bias_sends + 1,
+            bias_arrival + 1,
+            lambda there: qkv_bias_line.at[there],
+            qkv_bias_final.at[z],
+        )
+        qkv_bias_final[z] = qkv_bias_line[z]
+
+    def up_out():
+        around(
+            out_sends, out_arrival, lambda to: up_held.at[z, rows_of(to, 64)], up_final.at[k]
+        )
+        up_final[k] = up_held[z, rows_of(k, 64)]
+
+    def qkv_out():
+        around(
+            out_sends + 1,
+            out_arrival + 1,
+            lambda to: qkv_held.at[z, rows_of(to, 64)],
+            qkv_final.at[k],
+        )
+        qkv_final[k] = qkv_held[z, rows_of(k, 64)]
+
+    def down_out():
+        down_grad_ref[...] = down_held[z]
+
+    def dense_out():
+        dense_grad_ref[...] = dense_mine[z]
+
+    def up_result():
+        three(out_arrival, up_final.at[pl.ds(0, 3)])
+        up_grad_ref[...] = up_final[...]
+
+    def qkv_result():
+        three(out_arrival + 1, qkv_final.at[pl.ds(0, 3)])
+        qkv_grad_ref[...] = qkv_final[...]
+
+    own = rows_of(me.q, 128)
+    def layer_out():
+        mixed = reduce_out.finish()
+        layer_out_ref[...] = (
+            x_all[own].astype(F32) + mixed + vec_ref[4:5, :] + vec_ref[5:6, :]
+        ).astype(BF16)
+
+    def norm_grads():
+        from_attn = reduce_attn.finish()
+        from_mlp = reduce_mlp.finish()
+        cotangent = g_all[own].astype(F32)
+        unit, rate = norm_rows(own)
+        sums_held[...] = jnp.zeros_like(sums_held)
+        for which, field in enumerate(
+            (from_attn * unit, from_attn, from_mlp * unit, from_mlp, cotangent)
+        ):
+            sums_held[which : which + 1, :] = jnp.sum(field, axis=0, keepdims=True)
+        wires.copy(sums_sends, sums_arrival, sums_held, sums_core, me.core).start()
+        pulled = from_attn * vec_ref[0:1, :] + from_mlp * vec_ref[2:3, :]
+        pulled = (
+            pulled
+            - jnp.mean(pulled, axis=-1, keepdims=True)
+            - unit * jnp.mean(pulled * unit, axis=-1, keepdims=True)
+        )
+        input_grad_ref[...] = (cotangent + rate * pulled).astype(BF16)
+
+    def sums_plane():
+        three(sums_arrival, sums_core)
+        sums_chip[...] = sums_held[...] + sums_core[...]
+        for which in range(3):
+            wires.copy(
+                sums_sends + 1,
+                sums_arrival + 1,
+                sums_chip,
+                sums_cross.at[which],
+                me.cross[which],
+            ).start()
+
+    def sums_send():
+        three(sums_arrival + 1, sums_cross)
+        sums_total[...] = sums_chip[...] + sums_cross[0] + sums_cross[1] + sums_cross[2]
+        along(
+            sums_sends + 2,
+            sums_arrival + 2,
+            lambda there: sums_total.at[:, rows_of(there, 256)],
+            sums_line.at[z],
+        )
+        sums_line[z] = sums_total[:, rows_of(z, 256)]
+
+    def small_result():
+        three(sums_arrival + 2, sums_line.at[pl.ds(0, 3)])
+        three(bias_arrival, up_bias_final.at[pl.ds(0, 3)])
+        three(bias_arrival + 1, qkv_bias_final.at[pl.ds(0, 3)])
+        sums = sums_line[0] + sums_line[1] + sums_line[2] + sums_line[3]
+        sums = jnp.where(k >= 2, sums[:, 128:], sums[:, :128])
+        small_out_ref[0:8, :] = pltpu.roll(sums, (128 - (me.q % 4) * 32) % 128, 1)
+        bias_sum = qkv_bias_final[0] + qkv_bias_final[1] + qkv_bias_final[2] + qkv_bias_final[3]
+        small_out_ref[8:16, :] = pltpu.roll(bias_sum, (128 - k * 32) % 128, 1)
+        small_out_ref[16:24, :] = (
+            up_bias_final[0] + up_bias_final[1] + up_bias_final[2] + up_bias_final[3]
+        )
+
+    def ends_of(body):
+        def outer(index, carry):
+            return body(index * (LINE - 1), carry)
+
+        return outer
+
+    small_line_done()
+    locals_done()
+    gather_g.start(0)
+    upa_start()
+    gather_g.start(1)
+    line_dense.relay(1, 1)
+    line_upa.relay(1, 1)
+    gather_small.forward(0)
+    gather_g.start(2)
+    gather_x.forward(0)
+    upb_start()
+    line_dense.relay(1, 2)
+    line_dense.relay(0, 1)
+    line_dense.finish(1)
+    down_outer()
+    line_upb.relay(1, 1)
+    line_upa.relay(0, 1)
+    qkv_send()
+    gather_small.forward(1)
+    line_upb.relay(0, 1)
+    line_dense.relay(0, 2)
+    gather_x.forward(1)
+    line_upa.relay(1, 2)
+    gather_g.forward(0)
+    gather_small.corner()
+    line_dense.finish(0)
+    gather_x.corner()
+    gather_small.finish()
+    line_upa.relay(0, 2)
+    dense_send()
+    line_upb.relay(1, 2)
+    gather_g.forward(1)
+    vectors()
+    gather_x.finish()
+    qkv_outer()
+    lax.fori_loop(0, 4, norm_block, 0)
+    lax.fori_loop(4, 8, norm_block, 0)
+    gather_g.corner()
+    line_upb.relay(0, 2)
+    line_upa.finish(0)
+    line_upb.finish(1)
+    qkv_start()
+    gather_g.finish()
+    dense_done()
+    line_upa.finish(1)
+    lax.fori_loop(0, 4, activate_a, 0)
+    lax.fori_loop(0, 2, ends_of(down_block), 0)
+    line_upb.finish(0)
+    reduce_down.slot(0, 0)
+    reduce_down.slot(1, 0)
+    lax.fori_loop(0, 4, activate_b, 0)
+    line_qkv.relay(1, 1)
+    lax.fori_loop(1, 3, down_block, 0)
+    line_qkv.relay(0, 1)
+    reduce_down.slot(0, 1)
+    reduce_down.slot(1, 1)
+    line_qkv.relay(1, 2)
+    line_qkv.relay(0, 2)
+    line_qkv.finish(1)
+    down_start()
+    line_qkv.finish(0)
+    reduce_down.slot(1, 2)
+    reduce_down.slot(0, 2)
+    lax.fori_loop(3, 4, attend, 0)
+    lax.fori_loop(0, 1, attend, 0)
+    lax.fori_loop(1, 2, attend, 0)
+    line_down.relay(0, 1)
+    lax.fori_loop(2, 3, attend, 0)
+    line_down.relay(1, 1)
+    reduce_attn.pair(0).start()
+    reduce_attn.pair(1).start()
+    dense_part()
+    lax.fori_loop(0, 2, ends_of(qkv_block), 0)
+    lax.fori_loop(1, 3, qkv_block, 0)
+    reduce_down.finish(0)
+    reduce_qkv.slot(0, 0)
+    reduce_qkv.slot(1, 0)
+    reduce_attn.middle()
+    reduce_qkv.slot(1, 1)
+    reduce_down.finish(1)
+    line_down.relay(1, 2)
+    reduce_qkv.slot(0, 1)
+    line_down.relay(0, 2)
+    reduce_attn.turn(0)
+    reduce_attn.turn(1)
+    reduce_qkv.slot(0, 2)
+    reduce_qkv.slot(1, 2)
+    line_down.finish(0)
+    dense_back()
+    reduce_dense.slot(0, 0)
+    reduce_dense.slot(1, 0)
+    line_down.finish(1)
+    lax.fori_loop(2, 4, feed_back, 0)
+    lax.fori_loop(0, 2, feed_back, 0)
+    lax.fori_loop(0, 2, ends_of(up_block), 0)
+    reduce_dense.slot(1, 1)
+    lax.fori_loop(0, 2, feed_in, 0)
+    reduce_dense.slot(0, 1)
+    reduce_mlp.pair(0).start()
+    lax.fori_loop(2, 4, feed_in, 0)
+    reduce_up.slot(0, 0)
+    reduce_up.slot(1, 0)
+    lax.fori_loop(0, 2, mix, 0)
+    reduce_qkv.finish(1)
+    reduce_mlp.pair(1).start()
+    reduce_qkv.finish(0)
+    qkv_out()
+    reduce_dense.slot(0, 2)
+    reduce_mlp.middle()
+    qkv_result()
+    reduce_dense.slot(1, 2)
+    lax.fori_loop(1, 3, up_block, 0)
+    lax.fori_loop(2, 4, mix, 0)
+    reduce_up.slot(0, 1)
+    reduce_mlp.turn(1)
+    reduce_up.slot(1, 1)
+    reduce_dense.finish(1)
+    reduce_out.pair(1).start()
+    reduce_mlp.turn(0)
+    reduce_dense.finish(0)
+    reduce_out.pair(0).start()
+    reduce_out.middle()
+    reduce_up.slot(1, 2)
+    up_bias_send()
+    reduce_out.turn(0)
+    dense_out()
+    reduce_up.slot(0, 2)
+    reduce_out.turn(1)
+    norm_grads()
+    down_out()
+    sums_plane()
+    reduce_up.finish(1)
+    reduce_up.finish(0)
+    up_out()
+    layer_out()
+    sums_send()
+    small_result()
+    up_result()
+
+    for send, view in (
+        (up_send, up_w.at[pl.ds(0, 192)]),
+        (qkv_sends, qkv_w.at[pl.ds(0, 192)]),
+        (small_send, small_line.at[pl.ds(0, 3)]),
+        (dense_sends, dense_w.at[pl.ds(0, 96)]),
+        (back_sends, dense_mine.at[pl.ds(0, 3)]),
+        (back_sends + 1, qkv_bias_line.at[pl.ds(0, 3)]),
+        (bias_sends, up_bias_final.at[pl.ds(0, 3)]),
+        (bias_sends + 1, qkv_bias_final.at[pl.ds(0, 3)]),
+        (out_sends, up_final.at[pl.ds(0, 3)]),
+        (out_sends + 1, qkv_final.at[pl.ds(0, 3)]),
+        (sums_sends, sums_core),
+        (sums_sends + 1, sums_cross),
+        (sums_sends + 2, sums_line.at[pl.ds(0, 3)]),
+    ):
+        wires.all_sent(send, view, me.core)
+    for item in (
+        gather_x,
+        gather_g,
+        gather_small,
+        line_dense,
+        line_qkv,
+        line_upa,
+        line_upb,
+        line_down,
+        reduce_attn,
+        reduce_out,
+        reduce_mlp,
+        reduce_qkv,
+        reduce_dense,
+        reduce_down,
+        reduce_up,
+    ):
+        item.drain()
+
+
+def final_kernel(
+    layer_out_ref,
+    input_grad_ref,
+    qkv_ref,
+    dense_ref,
+    up_ref,
+    down_ref,
+    small_ref,
+    layer_out,
+    input_grad,
+    attn_gain_grad,
+    attn_shift_grad,
+    mlp_gain_grad,
+    mlp_shift_grad,
+    qkv_grad,
+    qkv_bias_grad,
+    dense_grad,
+    dense_bias_grad,
+    up_grad,
+    up_bias_grad,
+    down_grad,
+    down_bias_grad,
+):
+    layer_out[...] = layer_out_ref[...]
+    input_grad[...] = input_grad_ref[...]
+    for row, out in enumerate((attn_gain_grad, attn_shift_grad, mlp_gain_grad, mlp_shift_grad)):
+        out[...] = small_ref[row, :32]
+    dense_bias_grad[...] = small_ref[4, :32]
+    down_bias_grad[...] = small_ref[4, :32]
+    qkv_bias_grad[...] = small_ref[8:11, :32]
+    up_bias_grad[...] = small_ref[16, :]
+    for origin in range(4):
+        for which in range(3):
+            qkv_grad[which, :, origin * PAIR : (origin + 1) * PAIR] = qkv_ref[
+                origin, :, which * PAIR : (which + 1) * PAIR
+            ].astype(F32)
+        for place, other in enumerate(SEATS):
+            first = (other * 4 + origin) * 128
+            up_grad[:, first : first + 128] = up_ref[
+                origin, :, place * 128 : (place + 1) * 128
+            ].astype(F32)
+    dense_grad[...] = dense_ref[...].astype(F32)
+    down_grad[...] = down_ref[...].astype(F32)
+
+
+def plane_layer(
+    hidden_in,
+    out_grad,
+    span_start,
+    span_length,
+    attn_gain,
+    attn_shift,
+    mlp_gain,
+    mlp_shift,
+    qkv_weight,
+    qkv_bias,
+    dense_weight,
+    dense_bias,
+    up_weight,
+    up_bias,
+    down_weight,
+    down_bias,
+):
+    vmem = pl.BlockSpec(memory_space=pltpu.VMEM)
+    anywhere = pl.BlockSpec(memory_space=pl.ANY)
+    tokens = 4 * SEQ
+    outs = pl.pallas_call(
+        layer_kernel,
+        out_shape=(
+            jax.ShapeDtypeStruct((128, WIDTH), BF16),
+            jax.ShapeDtypeStruct((128, WIDTH), BF16),
+            jax.ShapeDtypeStruct((4, 64, 3 * PAIR), BF16),
+            jax.ShapeDtypeStruct((32, WIDTH), BF16),
+            jax.ShapeDtypeStruct((4, 64, HID), BF16),
+            jax.ShapeDtypeStruct((128, WIDTH), BF16),
+            jax.ShapeDtypeStruct((24, 128), F32),
+        ),
+        in_specs=[anywhere] * 7 + [vmem] * 10,
+        out_specs=(vmem,) * 7,
+        scratch_shapes=[
+            pltpu.VMEM((3, SEQ, PAIR), F32),
+            pltpu.VMEM((tokens, WIDTH), BF16),
+            pltpu.VMEM((tokens, WIDTH), BF16),
+            pltpu.VMEM((LINE, 8, 128), F32),
+            pltpu.VMEM((8, LINE, 8, 128), F32),
+            pltpu.VMEM((WIDTH, 3 * PAIR), BF16),
+            pltpu.VMEM((PAIR, WIDTH), BF16),
+            pltpu.VMEM((WIDTH, HID), BF16),
+            pltpu.VMEM((HID, WIDTH), BF16),
+            pltpu.VMEM((8, WIDTH), F32),
+            pltpu.VMEM((8, 3 * PAIR), F32),
+            pltpu.VMEM((tokens, WIDTH), BF16),
+            pltpu.VMEM((tokens, WIDTH), BF16),
+            pltpu.VMEM((tokens, PAIR), BF16),
+            pltpu.VMEM((tokens, 3 * PAIR), BF16),
+            pltpu.VMEM((tokens, HID), BF16),
+            pltpu.VMEM((tokens, HID), BF16),
+            pltpu.VMEM((tokens, HID), F32),
+            pltpu.VMEM((tokens, WIDTH), BF16),
+            pltpu.VMEM((tokens, WIDTH), BF16),
+            pltpu.VMEM((tokens, WIDTH), BF16),
+            pltpu.VMEM((3, 2, SEQ, WIDTH), BF16),
+            pltpu.VMEM((3, 3, 128, WIDTH), BF16),
+            pltpu.VMEM((LINE, 256, HID), BF16),
+            pltpu.VMEM((2, LINE, 256, HID), BF16),
+            pltpu.VMEM((LINE, 128, WIDTH), BF16),
+            pltpu.VMEM((2, LINE, 128, WIDTH), BF16),
+            pltpu.VMEM((LINE, 256, 3 * PAIR), BF16),
+            pltpu.VMEM((2, LINE, 256, 3 * PAIR), BF16),
+            pltpu.VMEM((4, 64, HID), BF16),
+            pltpu.VMEM((4, 64, 3 * PAIR), BF16),
+            pltpu.VMEM((LINE, 32, WIDTH), BF16),
+            pltpu.VMEM((PAIR, WIDTH), BF16),
+            pltpu.VMEM((LINE, 32, WIDTH), BF16),
+            pltpu.VMEM((2, LINE, 32, WIDTH), BF16),
+            pltpu.VMEM((8, PAIR), F32),
+            pltpu.VMEM((4, 8, PAIR), F32),
+            pltpu.VMEM((LINE, 8, PAIR), F32),
+            pltpu.VMEM((8, HID), F32),
+            pltpu.VMEM((LINE, 8, 128), F32),
+            pltpu.VMEM((8, WIDTH), F32),
+            pltpu.VMEM((8, WIDTH), F32),
+            pltpu.VMEM((8, WIDTH), F32),
+            pltpu.VMEM((8, WIDTH), F32),
+            pltpu.VMEM((3, 8, WIDTH), F32),
+            pltpu.VMEM((LINE, 8, 256), F32),
+            pltpu.SemaphoreType.DMA((37,)),
+            pltpu.SemaphoreType.DMA((92,)),
+            pltpu.SemaphoreType.DMA((14,)),
+        ],
+        compiler_params=pltpu.CompilerParams(
+            collective_id=0, has_side_effects=True, vmem_limit_bytes=60 * 2**20
+        ),
+    )(
+        hidden_in,
+        out_grad,
+        jnp.transpose(qkv_weight, (1, 0, 2)),
+        dense_weight,
+        up_weight,
+        down_weight,
+        jnp.asarray(turn_tables()),
+        attn_gain,
+        attn_shift,
+        mlp_gain,
+        mlp_shift,
+        dense_bias,
+        down_bias,
+        span_start,
+        span_length,
+        qkv_bias,
+        up_bias,
+    )
+    wide = jax.ShapeDtypeStruct((32,), F32)
+    finals = pl.pallas_call(
+        final_kernel,
+        out_shape=(
+            jax.ShapeDtypeStruct((128, WIDTH), BF16),
+            jax.ShapeDtypeStruct((128, WIDTH), BF16),
+            wide,
+            wide,
+            wide,
+            wide,
+            jax.ShapeDtypeStruct((3, 64, 512), F32),
+            jax.ShapeDtypeStruct((3, 32), F32),
+            jax.ShapeDtypeStruct((32, WIDTH), F32),
+            wide,
+            jax.ShapeDtypeStruct((64, 2048), F32),
+            jax.ShapeDtypeStruct((128,), F32),
+            jax.ShapeDtypeStruct((128, WIDTH), F32),
+            wide,
+        ),
+        in_specs=[vmem] * 7,
+        out_specs=(vmem,) * 14,
+    )(*outs)
+    return (*finals[:6], jnp.transpose(finals[6], (1, 0, 2)), *finals[7:])
+
+
 def solution(mesh):
     in_specs = (
         P(("dp", "tensor"), None),
@@ -296,4 +1566,5 @@
         P(("tensor", "dp"), None),
         P(("dp", "tensor")),
     )
-    return jax.shard_map(shards, mesh=mesh, in_specs=in_specs, out_specs=out_specs, check_vma=False)
+    fast = mesh.shape["dp"] == 16 and mesh.shape["tensor"] == 2
+    return jax.shard_map(plane_layer if fast else shards, mesh=mesh, in_specs=in_specs, out_specs=out_specs, check_vma=False)

time: 705 us -> 116 us (0.16)
  waiting for transfers between devices: 425 us -> 0 us
  blocking collectives: 176 us -> 0 us
  Pallas kernels: 0 us -> 115 us
  matrix products: 48.5 us -> 0 us
  local copies, waits for them, and re-layouts: 24.5 us -> 0 us
  other arithmetic: 14.6 us -> 0 us
  between operations: 15 us -> 0.67 us
    reduce_scatter x8 -> x0, waiting for transfers between devices: 359 us -> none  [the longest x1 109 us: shards(): lax.psum_scatter(up_grad, 'dp', scatter_dimension=0, tiled=True)]
    pallas_call x0 -> x2, Pallas kernels: none -> 115 us  [the longest x1 113 us: plane_layer(): pl.pallas_call(layer_kernel, out_shape=(jax.ShapeDtypeStruct((128, WIDTH)...]
    unnamed x3 -> x0, blocking collectives: 112 us -> none
    all_gather x5 -> x0, blocking collectives: 64.2 us -> none  [the longest x1 21.3 us: shards(): lax.all_gather(qkv_bias, 'dp', axis=1, tiled=True)]
    dot_general x18 -> x0, matrix products: 48.5 us -> none  [the longest x1 9.03 us: shards(): jnp.einsum('ld,fd->lf', cot_full, full_down, preferred_element_type=jnp.f...]
    all_gather x4 -> x0, waiting for transfers between devices: 44.1 us -> none  [the longest x1 44.1 us: shards(): lax.all_gather(down_weight, 'dp', axis=0, tiled=True)]
    unnamed x14 -> x0, waiting for transfers between devices: 21 us -> none
    unnamed x56 -> x0, local copies, waits for them, and re-layouts: 16.8 us -> none
  transfers between devices with their start and end apart: 13 -> 0, of which waited for: 9 -> 0; matrix products, arithmetic and copies ran while one was open for 12% -> 0% of each run, Pallas kernels for 0% -> 0%
where the time goes in v2:
time: 116 us
  Pallas kernels  115 us (99%)
    pallas_call x1, Pallas kernels, plane_layer(): pl.pallas_call(layer_kernel, out_shape=(jax.ShapeDtypeStruct((128, WIDTH)...  113 us
    pallas_call x1, Pallas kernels, plane_layer(): pl.pallas_call(final_kernel, out_shape=(jax.ShapeDtypeStruct((128, WIDTH)...  2.66 us

profile of v2, /device:TPU:0, one launch (start us, length us, event | category | flops | bytes accessed | tf_op | source)
XLA Modules:
  0.0 115.9 jit_solution(10342859081121456847)
XLA Ops:
  0.7 112.6 %shard_map.272 = (bf16[128,1024]{1,0:T(8,128)(2,1)}, bf16[128,1024]{1,0:T(8,128)(2,1)}, bf16[4,64,384]{2,1,0:T(8,128)(2,1)}, bf16[32,1024]{1,0:T(8,128)(2,1)}, b...) custom-call(bf16[128,1024]{1,0:T(8,128)(2,1)} %x_hbm.1, bf16[128,1024]{1,0:T(8,128)(2,1)} %g_hbm.1, ...), custom_call_target="tpu_custom_call" | custom-call | tf_op jit(solution)/shard_map/pallas_call | solution.py:1423
  113.3 2.7 %shard_map.273 = (bf16[128,1024]{1,0:T(8,128)(2,1)}, bf16[128,1024]{1,0:T(8,128)(2,1)}, f32[32]{0:T(128)}, f32[32]{0:T(128)}, f32[32]{0:T(128)}, /*index=5*/f32[...) custom-call(bf16[128,1024]{1,0:T(8,128)(2,1)} %get-tuple-element.35., ...), custom_call_target="tpu_custom_call" | custom-call | tf_op jit(solution)/shard_map/pallas_call | solution.py:1510

commit v3 on v2

--- a/solution.py
+++ b/solution.py
@@ -1179,144 +1179,144 @@
 
         return outer
 
+    locals_done()
+    upa_start()
+    line_dense.relay(0, 1)
+    upb_start()
     small_line_done()
-    locals_done()
+    qkv_send()
     gather_g.start(0)
-    upa_start()
-    gather_g.start(1)
     line_dense.relay(1, 1)
     line_upa.relay(1, 1)
+    line_upa.relay(0, 1)
+    qkv_outer()
+    qkv_start()
     gather_small.forward(0)
+    line_upb.relay(0, 1)
+    gather_x.forward(0)
+    line_dense.relay(1, 2)
+    gather_small.forward(1)
+    gather_g.start(1)
+    line_upb.relay(1, 1)
+    gather_x.forward(1)
+    gather_x.corner()
+    line_upa.relay(0, 2)
+    gather_small.corner()
+    gather_small.finish()
+    gather_g.forward(0)
+    line_upa.finish(0)
+    line_dense.relay(0, 2)
+    line_qkv.relay(1, 1)
+    line_dense.finish(1)
+    gather_g.forward(1)
+    line_dense.finish(0)
+    line_qkv.relay(0, 1)
+    vectors()
+    line_upb.relay(1, 2)
+    gather_x.finish()
+    dense_send()
+    line_upb.relay(0, 2)
+    line_upa.relay(1, 2)
     gather_g.start(2)
-    gather_x.forward(0)
-    upb_start()
-    line_dense.relay(1, 2)
-    line_dense.relay(0, 1)
-    line_dense.finish(1)
     down_outer()
-    line_upb.relay(1, 1)
-    line_upa.relay(0, 1)
-    qkv_send()
-    gather_small.forward(1)
-    line_upb.relay(0, 1)
-    line_dense.relay(0, 2)
-    gather_x.forward(1)
-    line_upa.relay(1, 2)
-    gather_g.forward(0)
-    gather_small.corner()
-    line_dense.finish(0)
-    gather_x.corner()
-    gather_small.finish()
-    line_upa.relay(0, 2)
-    dense_send()
-    line_upb.relay(1, 2)
-    gather_g.forward(1)
-    vectors()
-    gather_x.finish()
-    qkv_outer()
+    gather_g.corner()
+    line_qkv.relay(0, 2)
+    lax.fori_loop(4, 8, norm_block, 0)
     lax.fori_loop(0, 4, norm_block, 0)
-    lax.fori_loop(4, 8, norm_block, 0)
-    gather_g.corner()
-    line_upb.relay(0, 2)
-    line_upa.finish(0)
+    line_qkv.relay(1, 2)
+    line_upa.finish(1)
+    line_upb.finish(0)
     line_upb.finish(1)
-    qkv_start()
+    lax.fori_loop(0, 4, activate_a, 0)
+    dense_done()
+    down_start()
     gather_g.finish()
-    dense_done()
-    line_upa.finish(1)
-    lax.fori_loop(0, 4, activate_a, 0)
+    lax.fori_loop(0, 4, activate_b, 0)
     lax.fori_loop(0, 2, ends_of(down_block), 0)
-    line_upb.finish(0)
+    line_qkv.finish(1)
+    line_qkv.finish(0)
+    reduce_down.slot(1, 0)
     reduce_down.slot(0, 0)
-    reduce_down.slot(1, 0)
-    lax.fori_loop(0, 4, activate_b, 0)
-    line_qkv.relay(1, 1)
+    lax.fori_loop(2, 3, attend, 0)
+    lax.fori_loop(1, 2, attend, 0)
+    line_down.relay(1, 1)
+    line_down.relay(0, 1)
     lax.fori_loop(1, 3, down_block, 0)
-    line_qkv.relay(0, 1)
     reduce_down.slot(0, 1)
+    lax.fori_loop(3, 4, attend, 0)
     reduce_down.slot(1, 1)
-    line_qkv.relay(1, 2)
-    line_qkv.relay(0, 2)
-    line_qkv.finish(1)
-    down_start()
-    line_qkv.finish(0)
-    reduce_down.slot(1, 2)
-    reduce_down.slot(0, 2)
-    lax.fori_loop(3, 4, attend, 0)
     lax.fori_loop(0, 1, attend, 0)
-    lax.fori_loop(1, 2, attend, 0)
-    line_down.relay(0, 1)
-    lax.fori_loop(2, 3, attend, 0)
-    line_down.relay(1, 1)
-    reduce_attn.pair(0).start()
-    reduce_attn.pair(1).start()
-    dense_part()
+    line_down.relay(1, 2)
+    line_down.relay(0, 2)
     lax.fori_loop(0, 2, ends_of(qkv_block), 0)
-    lax.fori_loop(1, 3, qkv_block, 0)
-    reduce_down.finish(0)
     reduce_qkv.slot(0, 0)
     reduce_qkv.slot(1, 0)
+    reduce_down.slot(0, 2)
+    dense_part()
+    lax.fori_loop(1, 3, qkv_block, 0)
+    line_down.finish(1)
+    line_down.finish(0)
+    lax.fori_loop(0, 2, feed_back, 0)
+    reduce_qkv.slot(0, 1)
+    reduce_qkv.slot(1, 1)
+    lax.fori_loop(2, 4, feed_back, 0)
+    reduce_attn.pair(0).start()
+    lax.fori_loop(0, 2, ends_of(up_block), 0)
+    reduce_up.slot(1, 0)
+    reduce_attn.pair(1).start()
+    lax.fori_loop(0, 2, mix, 0)
     reduce_attn.middle()
-    reduce_qkv.slot(1, 1)
+    reduce_up.slot(0, 0)
+    reduce_out.pair(0).start()
+    dense_back()
+    lax.fori_loop(2, 4, mix, 0)
+    reduce_out.pair(1).start()
+    lax.fori_loop(2, 4, feed_in, 0)
+    reduce_qkv.slot(1, 2)
+    reduce_out.middle()
+    reduce_qkv.slot(0, 2)
+    reduce_attn.turn(0)
+    reduce_down.finish(0)
+    lax.fori_loop(0, 2, feed_in, 0)
+    lax.fori_loop(1, 3, up_block, 0)
+    reduce_mlp.pair(1).start()
+    reduce_mlp.pair(0).start()
+    reduce_dense.slot(1, 0)
+    reduce_up.slot(1, 1)
+    reduce_up.slot(0, 1)
+    reduce_qkv.finish(1)
+    reduce_dense.slot(0, 0)
+    up_bias_send()
+    reduce_dense.slot(1, 1)
+    reduce_mlp.middle()
+    reduce_attn.turn(1)
+    reduce_up.slot(1, 2)
+    reduce_mlp.turn(0)
+    reduce_mlp.turn(1)
+    reduce_out.turn(1)
+    reduce_qkv.finish(0)
+    reduce_down.slot(1, 2)
+    reduce_dense.slot(1, 2)
+    reduce_up.slot(0, 2)
+    reduce_out.turn(0)
+    reduce_dense.slot(0, 1)
+    qkv_out()
+    norm_grads()
+    reduce_up.finish(1)
+    sums_plane()
+    reduce_up.finish(0)
+    layer_out()
+    up_out()
+    reduce_dense.slot(0, 2)
+    sums_send()
+    reduce_dense.finish(0)
+    qkv_result()
     reduce_down.finish(1)
-    line_down.relay(1, 2)
-    reduce_qkv.slot(0, 1)
-    line_down.relay(0, 2)
-    reduce_attn.turn(0)
-    reduce_attn.turn(1)
-    reduce_qkv.slot(0, 2)
-    reduce_qkv.slot(1, 2)
-    line_down.finish(0)
-    dense_back()
-    reduce_dense.slot(0, 0)
-    reduce_dense.slot(1, 0)
-    line_down.finish(1)
-    lax.fori_loop(2, 4, feed_back, 0)
-    lax.fori_loop(0, 2, feed_back, 0)
-    lax.fori_loop(0, 2, ends_of(up_block), 0)
-    reduce_dense.slot(1, 1)
-    lax.fori_loop(0, 2, feed_in, 0)
-    reduce_dense.slot(0, 1)
-    reduce_mlp.pair(0).start()
-    lax.fori_loop(2, 4, feed_in, 0)
-    reduce_up.slot(0, 0)
-    reduce_up.slot(1, 0)
-    lax.fori_loop(0, 2, mix, 0)
-    reduce_qkv.finish(1)
-    reduce_mlp.pair(1).start()
-    reduce_qkv.finish(0)
-    qkv_out()
-    reduce_dense.slot(0, 2)
-    reduce_mlp.middle()
-    qkv_result()
-    reduce_dense.slot(1, 2)
-    lax.fori_loop(1, 3, up_block, 0)
-    lax.fori_loop(2, 4, mix, 0)
-    reduce_up.slot(0, 1)
-    reduce_mlp.turn(1)
-    reduce_up.slot(1, 1)
+    down_out()
     reduce_dense.finish(1)
-    reduce_out.pair(1).start()
-    reduce_mlp.turn(0)
-    reduce_dense.finish(0)
-    reduce_out.pair(0).start()
-    reduce_out.middle()
-    reduce_up.slot(1, 2)
-    up_bias_send()
-    reduce_out.turn(0)
+    up_result()
+    small_result()
     dense_out()
-    reduce_up.slot(0, 2)
-    reduce_out.turn(1)
-    norm_grads()
-    down_out()
-    sums_plane()
-    reduce_up.finish(1)
-    reduce_up.finish(0)
-    up_out()
-    layer_out()
-    sums_send()
-    small_result()
-    up_result()
 
     for send, view in (
         (up_send, up_w.at[pl.ds(0, 192)]),

time: 116 us -> 109 us (0.940)
  Pallas kernels: 115 us -> 108 us
    pallas_call x1, Pallas kernels: 113 us -> 106 us  [plane_layer(): pl.pallas_call(layer_kernel, out_shape=(jax.ShapeDtypeStruct((128, WIDTH)...]
where the time goes in v3:
time: 109 us
  Pallas kernels  108 us (99%)
    pallas_call x1, Pallas kernels, plane_layer(): pl.pallas_call(layer_kernel, out_shape=(jax.ShapeDtypeStruct((128, WIDTH)...  106 us
    pallas_call x1, Pallas kernels, plane_layer(): pl.pallas_call(final_kernel, out_shape=(jax.ShapeDtypeStruct((128, WIDTH)...  2.66 us

profile of v3, /device:TPU:0, one launch (start us, length us, event | category | flops | bytes accessed | tf_op | source)
XLA Modules:
  0.0 109.0 jit_solution(13535872831992505098)
XLA Ops:
  0.7 105.7 %shard_map.272 = (bf16[128,1024]{1,0:T(8,128)(2,1)}, bf16[128,1024]{1,0:T(8,128)(2,1)}, bf16[4,64,384]{2,1,0:T(8,128)(2,1)}, bf16[32,1024]{1,0:T(8,128)(2,1)}, b...) custom-call(bf16[128,1024]{1,0:T(8,128)(2,1)} %x_hbm.1, bf16[128,1024]{1,0:T(8,128)(2,1)} %g_hbm.1, ...), custom_call_target="tpu_custom_call" | custom-call | tf_op jit(solution)/shard_map/pallas_call | solution.py:1423
  106.3 2.7 %shard_map.273 = (bf16[128,1024]{1,0:T(8,128)(2,1)}, bf16[128,1024]{1,0:T(8,128)(2,1)}, f32[32]{0:T(128)}, f32[32]{0:T(128)}, f32[32]{0:T(128)}, /*index=5*/f32[...) custom-call(bf16[128,1024]{1,0:T(8,128)(2,1)} %get-tuple-element.35., ...), custom_call_target="tpu_custom_call" | custom-call | tf_op jit(solution)/shard_map/pallas_call | solution.py:1510

commit v4 on v3

--- a/solution.py
+++ b/solution.py
@@ -832,8 +832,13 @@
     def norm_block(block, carry):
         rows = rows_of(block, 128)
         unit, _ = norm_rows(rows)
+        normed_m[rows] = (unit * vec_ref[2:3, :] + vec_ref[3:4, :]).astype(BF16)
+        return carry
+
+    def attn_norm(block, carry):
+        rows = rows_of(block, 128)
+        unit, _ = norm_rows(rows)
         normed_a[rows] = (unit * vec_ref[0:1, :] + vec_ref[1:2, :]).astype(BF16)
-        normed_m[rows] = (unit * vec_ref[2:3, :] + vec_ref[3:4, :]).astype(BF16)
         return carry
 
     def activate(half):
@@ -955,6 +960,10 @@
             qkv_bias_held[which : which + 1, :] += jnp.sum(
                 grads[which].astype(F32), axis=0, keepdims=True
             )
+        return carry
+
+    def attend_in(tile, carry):
+        rows = rows_of(tile, 256)
         part_attn[rows] = nt(turned_grad[rows], qkv_w[...]).astype(BF16)
         return carry
 
@@ -1026,32 +1035,39 @@
         three(dense_arrival, dense_w.at[pl.ds(0, 96)])
         own_dense.wait()
 
+    def spread_table(kind, width):
+        table = small_all[...].reshape(256, 128).astype(BF16)
+        line_id = lax.broadcasted_iota(jnp.int32, (256, width), 0)
+        column = lax.broadcasted_iota(jnp.int32, (256, width), 1)
+        from_z, from_q = (line_id >> 3) & 3, line_id >> 5
+        if width == WIDTH:
+            chosen = from_z * 8 + from_q == column >> 5
+        else:
+            chosen = (from_z == k) & (from_q == (column >> 5) * 2 + t)
+        chosen = chosen & ((line_id & 7) == kind)
+        spread = tn(table, jnp.where(chosen, 1.0, 0.0).astype(BF16))
+        lane_row = lax.broadcasted_iota(jnp.int32, (128, width), 0)
+        lane_col = lax.broadcasted_iota(jnp.int32, (128, width), 1) & 31
+
+        def vector(which):
+            picked = jnp.where(lane_row == lane_col + which * 32, spread, 0.0)
+            return jnp.sum(picked, axis=0, keepdims=True)
+
+        return vector
+
     def vectors():
         own_small.wait()
-        table = small_all[...].reshape(256, 128).astype(BF16)
-        line_id = lax.broadcasted_iota(jnp.int32, (256, WIDTH), 0)
-        column = lax.broadcasted_iota(jnp.int32, (256, WIDTH), 1)
-        owner = ((line_id >> 3) & 3) * 8 + (line_id >> 5)
-        lane_row = lax.broadcasted_iota(jnp.int32, (128, WIDTH), 0)
-        lane_col = lax.broadcasted_iota(jnp.int32, (128, WIDTH), 1) & 31
-        for kind, count, base in ((0, 4, 0), (1, 2, 4)):
-            chosen = (owner == (column >> 5)) & ((line_id & 7) == kind)
-            spread = tn(table, jnp.where(chosen, 1.0, 0.0).astype(BF16))
-            for which in range(count):
-                picked = jnp.where(lane_row == lane_col + which * 32, spread, 0.0)
-                vec_ref[base + which : base + which + 1, :] = jnp.sum(picked, axis=0, keepdims=True)
-        line_id = line_id[:, :PAIR]
-        column = column[:, :PAIR]
-        chosen = (
-            (((line_id >> 3) & 3) == k)
-            & ((line_id >> 5) == (column >> 5) * 2 + t)
-            & ((line_id & 7) == 2)
-        )
-        spread = tn(table, jnp.where(chosen, 1.0, 0.0).astype(BF16))
+        vector = spread_table(0, WIDTH)
+        for which in range(4):
+            vec_ref[which : which + 1, :] = vector(which)
+
+    def more_vectors():
+        vector = spread_table(1, WIDTH)
+        for which in range(2):
+            vec_ref[4 + which : 5 + which, :] = vector(which)
+        vector = spread_table(2, PAIR)
         for which in range(3):
-            picked = jnp.where(lane_row[:, :PAIR] == lane_col[:, :PAIR] + which * 32, spread, 0.0)
-            total = jnp.sum(picked, axis=0, keepdims=True)
-            bias_ref[0:1, which * PAIR : (which + 1) * PAIR] = total
+            bias_ref[0:1, which * PAIR : (which + 1) * PAIR] = vector(which)
 
     def up_bias_send():
         along(
@@ -1181,141 +1197,146 @@
 
     locals_done()
     upa_start()
-    line_dense.relay(0, 1)
     upb_start()
     small_line_done()
     qkv_send()
+    line_dense.relay(0, 1)
+    line_upa.relay(1, 1)
     gather_g.start(0)
+    line_upa.relay(0, 1)
+    gather_g.start(1)
+    gather_x.forward(0)
     line_dense.relay(1, 1)
-    line_upa.relay(1, 1)
-    line_upa.relay(0, 1)
+    gather_g.start(2)
+    line_upb.relay(1, 1)
+    gather_x.forward(1)
     qkv_outer()
     qkv_start()
+    line_upb.relay(0, 1)
+    line_upb.relay(1, 2)
+    gather_small.forward(1)
+    down_outer()
+    line_dense.relay(1, 2)
     gather_small.forward(0)
-    line_upb.relay(0, 1)
-    gather_x.forward(0)
-    line_dense.relay(1, 2)
-    gather_small.forward(1)
-    gather_g.start(1)
-    line_upb.relay(1, 1)
-    gather_x.forward(1)
+    line_upa.relay(0, 2)
+    line_upa.relay(1, 2)
     gather_x.corner()
-    line_upa.relay(0, 2)
+    gather_g.forward(1)
+    line_upb.finish(1)
+    gather_g.forward(0)
+    line_dense.finish(1)
     gather_small.corner()
+    line_dense.relay(0, 2)
     gather_small.finish()
-    gather_g.forward(0)
+    gather_x.finish()
+    line_qkv.relay(1, 1)
+    line_qkv.relay(0, 1)
+    line_upb.relay(0, 2)
     line_upa.finish(0)
-    line_dense.relay(0, 2)
-    line_qkv.relay(1, 1)
-    line_dense.finish(1)
-    gather_g.forward(1)
+    vectors()
+    lax.fori_loop(4, 8, norm_block, 0)
+    gather_g.corner()
     line_dense.finish(0)
-    line_qkv.relay(0, 1)
-    vectors()
-    line_upb.relay(1, 2)
-    gather_x.finish()
+    line_upa.finish(1)
     dense_send()
-    line_upb.relay(0, 2)
-    line_upa.relay(1, 2)
-    gather_g.start(2)
-    down_outer()
-    gather_g.corner()
+    gather_g.finish()
+    lax.fori_loop(0, 4, norm_block, 0)
+    lax.fori_loop(0, 4, attn_norm, 0)
+    lax.fori_loop(4, 8, attn_norm, 0)
+    more_vectors()
+    lax.fori_loop(0, 4, activate_a, 0)
     line_qkv.relay(0, 2)
-    lax.fori_loop(4, 8, norm_block, 0)
-    lax.fori_loop(0, 4, norm_block, 0)
+    lax.fori_loop(0, 2, ends_of(down_block), 0)
     line_qkv.relay(1, 2)
-    line_upa.finish(1)
+    reduce_down.slot(0, 0)
     line_upb.finish(0)
-    line_upb.finish(1)
-    lax.fori_loop(0, 4, activate_a, 0)
+    down_start()
+    reduce_down.slot(1, 0)
     dense_done()
-    down_start()
-    gather_g.finish()
     lax.fori_loop(0, 4, activate_b, 0)
-    lax.fori_loop(0, 2, ends_of(down_block), 0)
+    lax.fori_loop(1, 3, down_block, 0)
     line_qkv.finish(1)
     line_qkv.finish(0)
-    reduce_down.slot(1, 0)
-    reduce_down.slot(0, 0)
-    lax.fori_loop(2, 3, attend, 0)
+    lax.fori_loop(0, 1, attend, 0)
     lax.fori_loop(1, 2, attend, 0)
+    lax.fori_loop(3, 4, attend, 0)
     line_down.relay(1, 1)
     line_down.relay(0, 1)
-    lax.fori_loop(1, 3, down_block, 0)
     reduce_down.slot(0, 1)
-    lax.fori_loop(3, 4, attend, 0)
     reduce_down.slot(1, 1)
-    lax.fori_loop(0, 1, attend, 0)
+    lax.fori_loop(2, 3, attend, 0)
+    lax.fori_loop(0, 2, attend_in, 0)
+    lax.fori_loop(2, 4, attend_in, 0)
+    lax.fori_loop(0, 2, ends_of(qkv_block), 0)
+    reduce_attn.pair(0).start()
+    reduce_attn.pair(1).start()
+    reduce_qkv.slot(0, 0)
     line_down.relay(1, 2)
+    reduce_qkv.slot(1, 0)
     line_down.relay(0, 2)
-    lax.fori_loop(0, 2, ends_of(qkv_block), 0)
-    reduce_qkv.slot(0, 0)
-    reduce_qkv.slot(1, 0)
+    reduce_attn.middle()
     reduce_down.slot(0, 2)
+    reduce_down.slot(1, 2)
     dense_part()
-    lax.fori_loop(1, 3, qkv_block, 0)
     line_down.finish(1)
     line_down.finish(0)
+    lax.fori_loop(2, 4, feed_back, 0)
+    lax.fori_loop(2, 4, feed_in, 0)
     lax.fori_loop(0, 2, feed_back, 0)
-    reduce_qkv.slot(0, 1)
-    reduce_qkv.slot(1, 1)
-    lax.fori_loop(2, 4, feed_back, 0)
-    reduce_attn.pair(0).start()
+    reduce_mlp.pair(1).start()
     lax.fori_loop(0, 2, ends_of(up_block), 0)
     reduce_up.slot(1, 0)
-    reduce_attn.pair(1).start()
+    reduce_up.slot(0, 0)
+    lax.fori_loop(0, 2, feed_in, 0)
+    lax.fori_loop(1, 3, qkv_block, 0)
+    lax.fori_loop(2, 4, mix, 0)
+    reduce_qkv.slot(1, 1)
+    reduce_qkv.slot(0, 1)
+    reduce_mlp.pair(0).start()
+    dense_back()
+    reduce_mlp.middle()
+    lax.fori_loop(1, 3, up_block, 0)
+    reduce_up.slot(0, 1)
+    reduce_attn.turn(1)
     lax.fori_loop(0, 2, mix, 0)
-    reduce_attn.middle()
-    reduce_up.slot(0, 0)
+    reduce_dense.slot(0, 0)
+    reduce_up.slot(1, 1)
+    reduce_mlp.turn(1)
+    reduce_attn.turn(0)
+    reduce_out.pair(1).start()
+    reduce_mlp.turn(0)
     reduce_out.pair(0).start()
-    dense_back()
-    lax.fori_loop(2, 4, mix, 0)
-    reduce_out.pair(1).start()
-    lax.fori_loop(2, 4, feed_in, 0)
     reduce_qkv.slot(1, 2)
     reduce_out.middle()
     reduce_qkv.slot(0, 2)
-    reduce_attn.turn(0)
+    reduce_dense.slot(1, 0)
+    reduce_up.slot(1, 2)
+    reduce_up.slot(0, 2)
+    reduce_dense.slot(0, 1)
+    norm_grads()
+    reduce_down.finish(1)
+    sums_plane()
     reduce_down.finish(0)
-    lax.fori_loop(0, 2, feed_in, 0)
-    lax.fori_loop(1, 3, up_block, 0)
-    reduce_mlp.pair(1).start()
-    reduce_mlp.pair(0).start()
-    reduce_dense.slot(1, 0)
-    reduce_up.slot(1, 1)
-    reduce_up.slot(0, 1)
     reduce_qkv.finish(1)
-    reduce_dense.slot(0, 0)
+    reduce_qkv.finish(0)
     up_bias_send()
+    reduce_out.turn(0)
     reduce_dense.slot(1, 1)
-    reduce_mlp.middle()
-    reduce_attn.turn(1)
-    reduce_up.slot(1, 2)
-    reduce_mlp.turn(0)
-    reduce_mlp.turn(1)
     reduce_out.turn(1)
-    reduce_qkv.finish(0)
-    reduce_down.slot(1, 2)
-    reduce_dense.slot(1, 2)
-    reduce_up.slot(0, 2)
-    reduce_out.turn(0)
-    reduce_dense.slot(0, 1)
     qkv_out()
-    norm_grads()
+    sums_send()
+    reduce_up.finish(0)
     reduce_up.finish(1)
-    sums_plane()
-    reduce_up.finish(0)
-    layer_out()
     up_out()
     reduce_dense.slot(0, 2)
-    sums_send()
+    down_out()
+    reduce_dense.slot(1, 2)
+    small_result()
+    qkv_result()
+    layer_out()
     reduce_dense.finish(0)
-    qkv_result()
-    reduce_down.finish(1)
-    down_out()
     reduce_dense.finish(1)
     up_result()
-    small_result()
     dense_out()
 
     for send, view in (

time: 109 us -> 106 us (0.972)
  Pallas kernels: 108 us -> 105 us
    pallas_call x1, Pallas kernels: 106 us -> 102 us  [plane_layer(): pl.pallas_call(layer_kernel, out_shape=(jax.ShapeDtypeStruct((128, WIDTH)...]
where the time goes in v4:
time: 106 us; the launch traced here: 105 us
  Pallas kernels  105 us (99%)
    pallas_call x1, Pallas kernels, plane_layer(): pl.pallas_call(layer_kernel, out_shape=(jax.ShapeDtypeStruct((128, WIDTH)...  102 us
    pallas_call x1, Pallas kernels, plane_layer(): pl.pallas_call(final_kernel, out_shape=(jax.ShapeDtypeStruct((128, WIDTH)...  2.66 us

profile of v4, /device:TPU:0, one launch (start us, length us, event | category | flops | bytes accessed | tf_op | source)
XLA Modules:
  0.0 105.4 jit_solution(6623730987723459157)
XLA Ops:
  0.7 102.0 %shard_map.272 = (bf16[128,1024]{1,0:T(8,128)(2,1)}, bf16[128,1024]{1,0:T(8,128)(2,1)}, bf16[4,64,384]{2,1,0:T(8,128)(2,1)}, bf16[32,1024]{1,0:T(8,128)(2,1)}, b...) custom-call(bf16[128,1024]{1,0:T(8,128)(2,1)} %x_hbm.1, bf16[128,1024]{1,0:T(8,128)(2,1)} %g_hbm.1, ...), custom_call_target="tpu_custom_call" | custom-call | tf_op jit(solution)/shard_map/pallas_call | solution.py:1444
  102.7 2.7 %shard_map.273 = (bf16[128,1024]{1,0:T(8,128)(2,1)}, bf16[128,1024]{1,0:T(8,128)(2,1)}, f32[32]{0:T(128)}, f32[32]{0:T(128)}, f32[32]{0:T(128)}, /*index=5*/f32[...) custom-call(bf16[128,1024]{1,0:T(8,128)(2,1)} %get-tuple-element.35., ...), custom_call_target="tpu_custom_call" | custom-call | tf_op jit(solution)/shard_map/pallas_call | solution.py:1531

commit v5 on v4

--- a/solution.py
+++ b/solution.py
@@ -624,6 +624,8 @@
     up_landed,
     down_held,
     down_landed,
+    late_held,
+    late_landed,
     qkv_held,
     qkv_landed,
     up_final,
@@ -784,6 +786,9 @@
     reduce_down = LineReduce(
         me, wires, down_held, down_landed
     )
+    reduce_late = LineReduce(
+        me, wires, late_held, late_landed
+    )
     reduce_up = LineReduce(
         me, wires, up_held, up_landed
     )
@@ -862,7 +867,9 @@
 
     def down_block(block, carry):
         units = rows_of(seat_of(block), 128)
-        down_held[block] = tn(active_ref[:, units], g_all[...]).astype(BF16)
+        grad = tn(active_ref[:, units], g_all[...]).astype(BF16)
+        down_held[block] = grad[:64]
+        late_held[block] = grad[64:]
         return carry
 
     def feed_back(tile, carry):
@@ -1114,7 +1121,8 @@
         qkv_final[k] = qkv_held[z, rows_of(k, 64)]
 
     def down_out():
-        down_grad_ref[...] = down_held[z]
+        down_grad_ref[0:64, :] = down_held[z]
+        down_grad_ref[64:128, :] = late_held[z]
 
     def dense_out():
         dense_grad_ref[...] = dense_mine[z]
@@ -1197,147 +1205,155 @@
 
     locals_done()
     upa_start()
+    line_dense.relay(1, 1)
     upb_start()
     small_line_done()
+    gather_g.start(0)
+    line_dense.relay(0, 1)
+    line_dense.relay(1, 2)
+    line_upa.relay(0, 1)
+    gather_small.forward(0)
     qkv_send()
-    line_dense.relay(0, 1)
     line_upa.relay(1, 1)
-    gather_g.start(0)
-    line_upa.relay(0, 1)
+    gather_x.forward(0)
+    line_upb.relay(0, 1)
+    gather_x.forward(1)
+    gather_small.forward(1)
+    qkv_outer()
+    down_outer()
+    line_upb.relay(1, 1)
+    line_dense.finish(1)
+    line_dense.relay(0, 2)
     gather_g.start(1)
-    gather_x.forward(0)
-    line_dense.relay(1, 1)
+    line_upa.relay(0, 2)
+    qkv_start()
+    gather_small.corner()
+    gather_x.corner()
+    gather_x.finish()
+    gather_small.finish()
+    vectors()
+    line_upb.relay(0, 2)
+    gather_g.forward(0)
+    line_upb.relay(1, 2)
+    line_dense.finish(0)
+    line_upa.finish(0)
+    line_upa.relay(1, 2)
+    lax.fori_loop(4, 8, attn_norm, 0)
     gather_g.start(2)
-    line_upb.relay(1, 1)
-    gather_x.forward(1)
-    qkv_outer()
-    qkv_start()
-    line_upb.relay(0, 1)
-    line_upb.relay(1, 2)
-    gather_small.forward(1)
-    down_outer()
-    line_dense.relay(1, 2)
-    gather_small.forward(0)
-    line_upa.relay(0, 2)
-    line_upa.relay(1, 2)
-    gather_x.corner()
+    lax.fori_loop(0, 4, attn_norm, 0)
+    line_qkv.relay(1, 1)
+    lax.fori_loop(4, 8, norm_block, 0)
     gather_g.forward(1)
+    line_qkv.relay(0, 1)
+    dense_send()
+    line_upb.finish(0)
+    lax.fori_loop(0, 4, norm_block, 0)
+    line_upa.finish(1)
     line_upb.finish(1)
-    gather_g.forward(0)
-    line_dense.finish(1)
-    gather_small.corner()
-    line_dense.relay(0, 2)
-    gather_small.finish()
-    gather_x.finish()
-    line_qkv.relay(1, 1)
-    line_qkv.relay(0, 1)
-    line_upb.relay(0, 2)
-    line_upa.finish(0)
-    vectors()
-    lax.fori_loop(4, 8, norm_block, 0)
+    lax.fori_loop(0, 4, activate_b, 0)
     gather_g.corner()
-    line_dense.finish(0)
-    line_upa.finish(1)
-    dense_send()
+    lax.fori_loop(0, 4, activate_a, 0)
+    line_qkv.relay(1, 2)
+    line_qkv.relay(0, 2)
     gather_g.finish()
-    lax.fori_loop(0, 4, norm_block, 0)
-    lax.fori_loop(0, 4, attn_norm, 0)
-    lax.fori_loop(4, 8, attn_norm, 0)
+    lax.fori_loop(0, 2, ends_of(down_block), 0)
+    dense_done()
+    lax.fori_loop(1, 3, down_block, 0)
+    reduce_down.slot(0, 0)
+    reduce_late.slot(0, 0)
+    reduce_down.slot(1, 0)
+    down_start()
     more_vectors()
-    lax.fori_loop(0, 4, activate_a, 0)
-    line_qkv.relay(0, 2)
-    lax.fori_loop(0, 2, ends_of(down_block), 0)
-    line_qkv.relay(1, 2)
-    reduce_down.slot(0, 0)
-    line_upb.finish(0)
-    down_start()
-    reduce_down.slot(1, 0)
-    dense_done()
-    lax.fori_loop(0, 4, activate_b, 0)
-    lax.fori_loop(1, 3, down_block, 0)
+    reduce_late.slot(1, 0)
+    line_qkv.finish(0)
     line_qkv.finish(1)
-    line_qkv.finish(0)
+    lax.fori_loop(3, 4, attend, 0)
     lax.fori_loop(0, 1, attend, 0)
+    lax.fori_loop(2, 3, attend, 0)
+    line_down.relay(0, 1)
+    reduce_down.slot(1, 1)
+    line_down.relay(1, 1)
+    reduce_down.slot(0, 1)
     lax.fori_loop(1, 2, attend, 0)
-    lax.fori_loop(3, 4, attend, 0)
-    line_down.relay(1, 1)
-    line_down.relay(0, 1)
-    reduce_down.slot(0, 1)
-    reduce_down.slot(1, 1)
-    lax.fori_loop(2, 3, attend, 0)
+    lax.fori_loop(0, 2, ends_of(qkv_block), 0)
+    reduce_qkv.slot(0, 0)
+    reduce_qkv.slot(1, 0)
+    reduce_late.slot(1, 1)
     lax.fori_loop(0, 2, attend_in, 0)
+    dense_part()
+    reduce_attn.pair(0).start()
+    reduce_late.slot(0, 1)
+    line_down.relay(1, 2)
+    line_down.relay(0, 2)
     lax.fori_loop(2, 4, attend_in, 0)
-    lax.fori_loop(0, 2, ends_of(qkv_block), 0)
-    reduce_attn.pair(0).start()
+    lax.fori_loop(1, 3, qkv_block, 0)
+    reduce_down.slot(0, 2)
     reduce_attn.pair(1).start()
-    reduce_qkv.slot(0, 0)
-    line_down.relay(1, 2)
-    reduce_qkv.slot(1, 0)
-    line_down.relay(0, 2)
-    reduce_attn.middle()
-    reduce_down.slot(0, 2)
-    reduce_down.slot(1, 2)
-    dense_part()
+    line_down.finish(0)
+    reduce_qkv.slot(0, 1)
+    dense_back()
+    reduce_qkv.slot(1, 1)
     line_down.finish(1)
-    line_down.finish(0)
+    lax.fori_loop(0, 2, feed_back, 0)
     lax.fori_loop(2, 4, feed_back, 0)
-    lax.fori_loop(2, 4, feed_in, 0)
-    lax.fori_loop(0, 2, feed_back, 0)
-    reduce_mlp.pair(1).start()
+    reduce_dense.slot(1, 0)
     lax.fori_loop(0, 2, ends_of(up_block), 0)
     reduce_up.slot(1, 0)
     reduce_up.slot(0, 0)
+    reduce_attn.middle()
     lax.fori_loop(0, 2, feed_in, 0)
-    lax.fori_loop(1, 3, qkv_block, 0)
+    lax.fori_loop(2, 4, feed_in, 0)
+    reduce_dense.slot(0, 0)
+    reduce_mlp.pair(1).start()
+    reduce_mlp.pair(0).start()
+    reduce_mlp.middle()
+    reduce_qkv.slot(1, 2)
+    reduce_qkv.slot(0, 2)
+    lax.fori_loop(1, 3, up_block, 0)
     lax.fori_loop(2, 4, mix, 0)
-    reduce_qkv.slot(1, 1)
-    reduce_qkv.slot(0, 1)
-    reduce_mlp.pair(0).start()
-    dense_back()
-    reduce_mlp.middle()
-    lax.fori_loop(1, 3, up_block, 0)
-    reduce_up.slot(0, 1)
-    reduce_attn.turn(1)
     lax.fori_loop(0, 2, mix, 0)
-    reduce_dense.slot(0, 0)
+    reduce_down.finish(0)
+    reduce_out.pair(1).start()
     reduce_up.slot(1, 1)
+    reduce_dense.slot(1, 1)
     reduce_mlp.turn(1)
     reduce_attn.turn(0)
-    reduce_out.pair(1).start()
+    reduce_down.slot(1, 2)
     reduce_mlp.turn(0)
     reduce_out.pair(0).start()
-    reduce_qkv.slot(1, 2)
+    reduce_attn.turn(1)
+    reduce_up.slot(0, 1)
     reduce_out.middle()
-    reduce_qkv.slot(0, 2)
-    reduce_dense.slot(1, 0)
+    reduce_qkv.finish(0)
     reduce_up.slot(1, 2)
-    reduce_up.slot(0, 2)
+    reduce_late.slot(1, 2)
     reduce_dense.slot(0, 1)
     norm_grads()
+    reduce_up.slot(0, 2)
+    reduce_dense.slot(1, 2)
+    reduce_late.slot(0, 2)
+    sums_plane()
+    reduce_qkv.finish(1)
+    qkv_out()
+    reduce_dense.slot(0, 2)
+    up_bias_send()
+    reduce_out.turn(1)
+    reduce_out.turn(0)
     reduce_down.finish(1)
-    sums_plane()
-    reduce_down.finish(0)
-    reduce_qkv.finish(1)
-    reduce_qkv.finish(0)
-    up_bias_send()
-    reduce_out.turn(0)
-    reduce_dense.slot(1, 1)
-    reduce_out.turn(1)
-    qkv_out()
     sums_send()
+    reduce_up.finish(1)
     reduce_up.finish(0)
-    reduce_up.finish(1)
     up_out()
-    reduce_dense.slot(0, 2)
+    layer_out()
+    reduce_late.finish(1)
+    reduce_late.finish(0)
+    qkv_result()
     down_out()
-    reduce_dense.slot(1, 2)
+    reduce_dense.finish(1)
+    reduce_dense.finish(0)
+    dense_out()
+    up_result()
     small_result()
-    qkv_result()
-    layer_out()
-    reduce_dense.finish(0)
-    reduce_dense.finish(1)
-    up_result()
-    dense_out()
 
     for send, view in (
         (up_send, up_w.at[pl.ds(0, 192)]),
@@ -1370,6 +1386,7 @@
         reduce_qkv,
         reduce_dense,
         reduce_down,
+        reduce_late,
         reduce_up,
     ):
         item.drain()
@@ -1480,8 +1497,10 @@
             pltpu.VMEM((3, 3, 128, WIDTH), BF16),
             pltpu.VMEM((LINE, 256, HID), BF16),
             pltpu.VMEM((2, LINE, 256, HID), BF16),
-            pltpu.VMEM((LINE, 128, WIDTH), BF16),
-            pltpu.VMEM((2, LINE, 128, WIDTH), BF16),
+            pltpu.VMEM((LINE, 64, WIDTH), BF16),
+            pltpu.VMEM((2, LINE, 64, WIDTH), BF16),
+            pltpu.VMEM((LINE, 64, WIDTH), BF16),
+            pltpu.VMEM((2, LINE, 64, WIDTH), BF16),
             pltpu.VMEM((LINE, 256, 3 * PAIR), BF16),
             pltpu.VMEM((2, LINE, 256, 3 * PAIR), BF16),
             pltpu.VMEM((4, 64, HID), BF16),
@@ -1501,8 +1520,8 @@
             pltpu.VMEM((8, WIDTH), F32),
             pltpu.VMEM((3, 8, WIDTH), F32),
             pltpu.VMEM((LINE, 8, 256), F32),
-            pltpu.SemaphoreType.DMA((37,)),
-            pltpu.SemaphoreType.DMA((92,)),
+            pltpu.SemaphoreType.DMA((39,)),
+            pltpu.SemaphoreType.DMA((98,)),
             pltpu.SemaphoreType.DMA((14,)),
         ],
         compiler_params=pltpu.CompilerParams(

time: 106 us -> 104 us (0.981)
  Pallas kernels: 105 us -> 103 us
    pallas_call x1, Pallas kernels: 102 us -> 101 us  [plane_layer(): pl.pallas_call(layer_kernel, out_shape=(jax.ShapeDtypeStruct((128, WIDTH)...]
where the time goes in v5:
time: 104 us
  Pallas kernels  103 us (99%)
    pallas_call x1, Pallas kernels, plane_layer(): pl.pallas_call(layer_kernel, out_shape=(jax.ShapeDtypeStruct((128, WIDTH)...  101 us
    pallas_call x1, Pallas kernels, plane_layer(): pl.pallas_call(final_kernel, out_shape=(jax.ShapeDtypeStruct((128, WIDTH)...  2.66 us

profile of v5, /device:TPU:0, one launch (start us, length us, event | category | flops | bytes accessed | tf_op | source)
XLA Modules:
  0.0 104.1 jit_solution(16040677104569785816)
XLA Ops:
  0.7 100.7 %shard_map.272 = (bf16[128,1024]{1,0:T(8,128)(2,1)}, bf16[128,1024]{1,0:T(8,128)(2,1)}, bf16[4,64,384]{2,1,0:T(8,128)(2,1)}, bf16[32,1024]{1,0:T(8,128)(2,1)}, b...) custom-call(bf16[128,1024]{1,0:T(8,128)(2,1)} %x_hbm.1, bf16[128,1024]{1,0:T(8,128)(2,1)} %g_hbm.1, ...), custom_call_target="tpu_custom_call" | custom-call | tf_op jit(solution)/shard_map/pallas_call | solution.py:1461
  101.4 2.7 %shard_map.273 = (bf16[128,1024]{1,0:T(8,128)(2,1)}, bf16[128,1024]{1,0:T(8,128)(2,1)}, f32[32]{0:T(128)}, f32[32]{0:T(128)}, f32[32]{0:T(128)}, /*index=5*/f32[...) custom-call(bf16[128,1024]{1,0:T(8,128)(2,1)} %get-tuple-element.35., ...), custom_call_target="tpu_custom_call" | custom-call | tf_op jit(solution)/shard_map/pallas_call | solution.py:1550

commit v6 on v5

--- a/solution.py
+++ b/solution.py
@@ -1234,9 +1234,9 @@
     vectors()
     line_upb.relay(0, 2)
     gather_g.forward(0)
-    line_upb.relay(1, 2)
     line_dense.finish(0)
     line_upa.finish(0)
+    line_upb.relay(1, 2)
     line_upa.relay(1, 2)
     lax.fori_loop(4, 8, attn_norm, 0)
     gather_g.start(2)
@@ -1253,8 +1253,8 @@
     lax.fori_loop(0, 4, activate_b, 0)
     gather_g.corner()
     lax.fori_loop(0, 4, activate_a, 0)
+    line_qkv.relay(0, 2)
     line_qkv.relay(1, 2)
-    line_qkv.relay(0, 2)
     gather_g.finish()
     lax.fori_loop(0, 2, ends_of(down_block), 0)
     dense_done()
@@ -1264,8 +1264,8 @@
     reduce_down.slot(1, 0)
     down_start()
     more_vectors()
+    line_qkv.finish(0)
     reduce_late.slot(1, 0)
-    line_qkv.finish(0)
     line_qkv.finish(1)
     lax.fori_loop(3, 4, attend, 0)
     lax.fori_loop(0, 1, attend, 0)
@@ -1282,8 +1282,8 @@
     lax.fori_loop(0, 2, attend_in, 0)
     dense_part()
     reduce_attn.pair(0).start()
+    line_down.relay(1, 2)
     reduce_late.slot(0, 1)
-    line_down.relay(1, 2)
     line_down.relay(0, 2)
     lax.fori_loop(2, 4, attend_in, 0)
     lax.fori_loop(1, 3, qkv_block, 0)
@@ -1298,29 +1298,29 @@
     lax.fori_loop(2, 4, feed_back, 0)
     reduce_dense.slot(1, 0)
     lax.fori_loop(0, 2, ends_of(up_block), 0)
+    reduce_up.slot(0, 0)
     reduce_up.slot(1, 0)
-    reduce_up.slot(0, 0)
     reduce_attn.middle()
+    lax.fori_loop(2, 4, feed_in, 0)
     lax.fori_loop(0, 2, feed_in, 0)
-    lax.fori_loop(2, 4, feed_in, 0)
     reduce_dense.slot(0, 0)
+    reduce_mlp.pair(0).start()
     reduce_mlp.pair(1).start()
-    reduce_mlp.pair(0).start()
     reduce_mlp.middle()
+    reduce_qkv.slot(0, 2)
     reduce_qkv.slot(1, 2)
-    reduce_qkv.slot(0, 2)
     lax.fori_loop(1, 3, up_block, 0)
+    lax.fori_loop(0, 2, mix, 0)
     lax.fori_loop(2, 4, mix, 0)
-    lax.fori_loop(0, 2, mix, 0)
     reduce_down.finish(0)
     reduce_out.pair(1).start()
     reduce_up.slot(1, 1)
     reduce_dense.slot(1, 1)
     reduce_mlp.turn(1)
+    reduce_out.pair(0).start()
     reduce_attn.turn(0)
     reduce_down.slot(1, 2)
     reduce_mlp.turn(0)
-    reduce_out.pair(0).start()
     reduce_attn.turn(1)
     reduce_up.slot(0, 1)
     reduce_out.middle()
@@ -1331,29 +1331,29 @@
     norm_grads()
     reduce_up.slot(0, 2)
     reduce_dense.slot(1, 2)
+    sums_plane()
     reduce_late.slot(0, 2)
-    sums_plane()
     reduce_qkv.finish(1)
+    reduce_out.turn(0)
     qkv_out()
     reduce_dense.slot(0, 2)
     up_bias_send()
     reduce_out.turn(1)
-    reduce_out.turn(0)
+    reduce_up.finish(1)
+    reduce_up.finish(0)
     reduce_down.finish(1)
     sums_send()
-    reduce_up.finish(1)
-    reduce_up.finish(0)
     up_out()
     layer_out()
     reduce_late.finish(1)
     reduce_late.finish(0)
-    qkv_result()
     down_out()
     reduce_dense.finish(1)
     reduce_dense.finish(0)
+    qkv_result()
+    small_result()
+    up_result()
     dense_out()
-    up_result()
-    small_result()
 
     for send, view in (
         (up_send, up_w.at[pl.ds(0, 192)]),

time: 104 us -> 104 us (level)
  no operation moved by 1% of the time
where the time goes in v6:
time: 104 us
  Pallas kernels  103 us (99%)
    pallas_call x1, Pallas kernels, plane_layer(): pl.pallas_call(layer_kernel, out_shape=(jax.ShapeDtypeStruct((128, WIDTH)...  101 us
    pallas_call x1, Pallas kernels, plane_layer(): pl.pallas_call(final_kernel, out_shape=(jax.ShapeDtypeStruct((128, WIDTH)...  2.66 us

profile of v6, /device:TPU:0, one launch (start us, length us, event | category | flops | bytes accessed | tf_op | source)
XLA Modules:
  0.0 104.1 jit_solution(6349110261180127638)
XLA Ops:
  0.7 100.8 %shard_map.272 = (bf16[128,1024]{1,0:T(8,128)(2,1)}, bf16[128,1024]{1,0:T(8,128)(2,1)}, bf16[4,64,384]{2,1,0:T(8,128)(2,1)}, bf16[32,1024]{1,0:T(8,128)(2,1)}, b...) custom-call(bf16[128,1024]{1,0:T(8,128)(2,1)} %x_hbm.1, bf16[128,1024]{1,0:T(8,128)(2,1)} %g_hbm.1, ...), custom_call_target="tpu_custom_call" | custom-call | tf_op jit(solution)/shard_map/pallas_call | solution.py:1461
  101.4 2.7 %shard_map.273 = (bf16[128,1024]{1,0:T(8,128)(2,1)}, bf16[128,1024]{1,0:T(8,128)(2,1)}, f32[32]{0:T(128)}, f32[32]{0:T(128)}, f32[32]{0:T(128)}, /*index=5*/f32[...) custom-call(bf16[128,1024]{1,0:T(8,128)(2,1)} %get-tuple-element.35., ...), custom_call_target="tpu_custom_call" | custom-call | tf_op jit(solution)/shard_map/pallas_call | solution.py:1550
